TPU v7x, 32 devices: a whole 2x2x4 slice. The times are simulated.
32 devices in a mesh: wshard: 8 (over z, y), seq: 4 (over x, core).
Axes of the slice: x: 2, y: 2, z: 4, core: 2. Of those that a mesh axis runs over, the one named last changes fastest.
Arguments:
- tokens: bfloat16 [24576, 768], P(('wshard', 'seq')), may hold values from -6 to 6
- cotangent: bfloat16 [24576, 768], P(('wshard', 'seq')), may hold values from -6 to 6
- starts: int32 [8, 8], P('wshard'), may hold values from 0 to 2688, as said below
- w_query: bfloat16 [768, 768], P('wshard'), may hold values from -0.21875 to 0.21875
- w_key: bfloat16 [768, 768], P('wshard'), may hold values from -0.21875 to 0.21875
- w_value: bfloat16 [768, 768], P('wshard'), may hold values from -0.21875 to 0.21875
- w_output: bfloat16 [768, 768], P('wshard'), may hold values from -1.25 to 1.25
- w_inner: bfloat16 [768, 3072], P('wshard'), may hold values from -0.21875 to 0.21875
- w_outer: bfloat16 [3072, 768], P('wshard'), may hold values from -0.109375 to 0.109375
- b_query: bfloat16 [768], P('wshard'), may hold values from -3 to 3
- b_value: bfloat16 [768], P('wshard'), may hold values from -3 to 3
- b_output: bfloat16 [768], P('wshard'), may hold values from -3 to 3
- b_inner: bfloat16 [3072], P('wshard'), may hold values from -3 to 3
- b_outer: bfloat16 [768], P('wshard'), may hold values from -3 to 3
- gain_first: bfloat16 [768], P('wshard'), may hold values from 0.5 to 2
- bias_first: bfloat16 [768], P('wshard'), may hold values from -3 to 3
- gain_second: bfloat16 [768], P('wshard'), may hold values from 0.5 to 2
- bias_second: bfloat16 [768], P('wshard'), may hold values from -3 to 3
Outputs:
- layer_out: bfloat16 [24576, 768], P(('wshard', 'seq'))
- grad_tokens: float32 [24576, 768], P(('wshard', 'seq'))
- grad_w_query: float32 [768, 768], P('wshard')
- grad_w_key: float32 [768, 768], P('wshard')
- grad_w_value: float32 [768, 768], P('wshard')
- grad_w_output: float32 [768, 768], P('wshard')
- grad_w_inner: float32 [768, 3072], P('wshard')
- grad_w_outer: float32 [3072, 768], P('wshard')
- grad_b_query: float32 [768], P('wshard')
- grad_b_value: float32 [768], P('wshard')
- grad_b_output: float32 [768], P('wshard')
- grad_b_inner: float32 [3072], P('wshard')
- grad_b_outer: float32 [768], P('wshard')
- grad_gain_first: float32 [768], P('wshard')
- grad_bias_first: float32 [768], P('wshard')
- grad_gain_second: float32 [768], P('wshard')
- grad_bias_second: float32 [768], P('wshard')
Inputs may be any that keep to these rules, and one draw needn't show every extreme that they name: `starts`: row w lists where the 8 documents of stream w begin: the first is 0 and they strictly increase; the last document of every stream holds exactly 384 positions; documents run across the devices of a stream.
All inputs are finite; a program needn't handle non-finite values.
Results may differ from a plain program's by a relative error of at most 0.017.
Values may be sent and summed in bfloat16 or wider, within the bound.
A program may use at most 192 MiB of HBM per device.

v0:
```python
import jax
import jax.numpy as jnp
from jax import lax
from jax.sharding import PartitionSpec as P

H = 12
HD = 64


NORM_EPS = 1e-05


def layer_norm(inputs, norm_gain, norm_bias):
    row_mean = jnp.mean(inputs, axis=-1, keepdims=True)
    centred = inputs - row_mean
    row_var = jnp.mean(centred * centred, axis=-1, keepdims=True)
    return centred * lax.rsqrt(row_var + NORM_EPS) * norm_gain + norm_bias


def gelu_exact(inputs):
    return jax.nn.gelu(inputs, approximate=False)


def contract(left_in, right_in, left_dim, right_dim):
    return lax.dot_general(
        left_in,
        right_in,
        (((left_dim,), (right_dim,)), ((), ())),
        preferred_element_type=jnp.float32,
    )


def join_blocks(blocks):
    return jnp.transpose(blocks, (1, 2, 0, 3)).reshape(blocks.shape[1] * blocks.shape[2], -1)


def shards(
    tokens,
    cotangent,
    starts,
    w_query,
    w_key,
    w_value,
    w_output,
    w_inner,
    w_outer,
    b_query,
    b_value,
    b_output,
    b_inner,
    b_outer,
    gain_first,
    bias_first,
    gain_second,
    bias_second,
):
    gathered = (
        lax.all_gather(w_query, "wshard", axis=0, tiled=True),
        lax.all_gather(w_key, "wshard", axis=0, tiled=True),
        lax.all_gather(w_value, "wshard", axis=0, tiled=True),
        lax.all_gather(w_output, "wshard", axis=0, tiled=True),
        lax.all_gather(w_inner, "wshard", axis=0, tiled=True),
        lax.all_gather(w_outer, "wshard", axis=0, tiled=True),
        lax.all_gather(b_query, "wshard", axis=0, tiled=True),
        lax.all_gather(b_value, "wshard", axis=0, tiled=True),
        lax.all_gather(b_output, "wshard", axis=0, tiled=True),
        lax.all_gather(b_inner, "wshard", axis=0, tiled=True),
        lax.all_gather(b_outer, "wshard", axis=0, tiled=True),
        lax.all_gather(gain_first, "wshard", axis=0, tiled=True),
        lax.all_gather(bias_first, "wshard", axis=0, tiled=True),
        lax.all_gather(gain_second, "wshard", axis=0, tiled=True),
        lax.all_gather(bias_second, "wshard", axis=0, tiled=True),
    )
    query_full, key_full, value_full, output_full, inner_full, outer_full = gathered[:6]
    small_full = [member.astype(jnp.float32) for member in gathered[6:]]
    (
        bias_query,
        bias_value,
        bias_output,
        bias_inner,
        bias_outer,
        norm_gain_one,
        norm_bias_one,
        norm_gain_two,
        norm_bias_two,
    ) = small_full
    local_heads = H // lax.axis_size("seq")
    head_size = HD
    score_scale = head_size ** (-0.5)
    q_tok = (contract(query_full, tokens, 0, 1) + bias_query[:, None]).astype(jnp.bfloat16)
    k_tok = contract(key_full, tokens, 0, 1).astype(jnp.bfloat16)
    v_tok = (contract(value_full, tokens, 0, 1) + bias_value[:, None]).astype(jnp.bfloat16)
    q_flat, k_flat, v_flat = (
        lax.all_to_all(q_tok, "seq", split_axis=0, concat_axis=1, tiled=True),
        lax.all_to_all(k_tok, "seq", split_axis=0, concat_axis=1, tiled=True),
        lax.all_to_all(v_tok, "seq", split_axis=0, concat_axis=1, tiled=True),
    )
    stream_len = q_flat.shape[1]
    q_heads = q_flat.reshape(local_heads, head_size, stream_len)
    k_heads = k_flat.reshape(local_heads, head_size, stream_len)
    v_heads = v_flat.reshape(local_heads, head_size, stream_len)
    positions = jnp.arange(stream_len, dtype=jnp.int32)
    segment = jnp.sum((starts[0][None, :] <= positions[:, None]).astype(jnp.int32), axis=1)
    block_rows = min(512, stream_len)
    block_count = stream_len // block_rows

    def block_scores(block_index):
        start_row = block_index * block_rows
        q_block = lax.dynamic_slice_in_dim(q_heads, start_row, block_rows, 2)
        seg_block = lax.dynamic_slice_in_dim(segment, start_row, block_rows, 0)
        scores = (
            jnp.einsum("hdq,hdk->hqk", q_block, k_heads, preferred_element_type=jnp.float32)
            * score_scale
        )
        allowed = seg_block[:, None] == segment[None, :]
        return (q_block, jnp.where(allowed[None], scores, -1e30))

    def forward_block(block_index):
        q_block, scores = block_scores(block_index)
        row_max = jnp.max(scores, axis=-1, keepdims=True)
        expo_vals = jnp.exp(scores - row_max)
        row_sum = jnp.sum(expo_vals, axis=-1, keepdims=True)
        probs_low = (expo_vals / row_sum).astype(jnp.bfloat16)
        mixed_block = jnp.einsum(
            "hqk,hdk->hdq", probs_low, v_heads, preferred_element_type=jnp.float32
        )
        return (mixed_block, (row_max + jnp.log(row_sum))[..., 0])

    mixed_blocks, lse_blocks = lax.map(forward_block, jnp.arange(block_count))
    mixed_heads = join_blocks(mixed_blocks).astype(jnp.bfloat16)
    log_sums = jnp.transpose(lse_blocks, (1, 0, 2)).reshape(local_heads, stream_len)
    mixed_tok = lax.all_to_all(mixed_heads, "seq", split_axis=1, concat_axis=0, tiled=True)
    attn_out = contract(mixed_tok, output_full, 0, 0) + bias_output
    residual_in = tokens.astype(jnp.float32) + attn_out
    first_norm, first_back = jax.vjp(layer_norm, residual_in, norm_gain_one, norm_bias_one)
    first_low = first_norm.astype(jnp.bfloat16)
    inner_act = jnp.dot(first_low, inner_full, preferred_element_type=jnp.float32) + bias_inner
    gelu_out, gelu_back = jax.vjp(gelu_exact, inner_act)
    gelu_low = gelu_out.astype(jnp.bfloat16)
    outer_act = jnp.dot(gelu_low, outer_full, preferred_element_type=jnp.float32) + bias_outer
    second_in = first_norm + outer_act
    layer_result, second_back = jax.vjp(layer_norm, second_in, norm_gain_two, norm_bias_two)
    layer_output = layer_result.astype(jnp.bfloat16)
    regathered = (
        lax.all_gather(w_query, "wshard", axis=0, tiled=True),
        lax.all_gather(w_key, "wshard", axis=0, tiled=True),
        lax.all_gather(w_value, "wshard", axis=0, tiled=True),
        lax.all_gather(w_output, "wshard", axis=0, tiled=True),
        lax.all_gather(w_inner, "wshard", axis=0, tiled=True),
        lax.all_gather(w_outer, "wshard", axis=0, tiled=True),
    )
    query_full, key_full, value_full, output_full, inner_full, outer_full = regathered
    d_second, grad_gain_two, grad_bias_two = second_back(cotangent.astype(jnp.float32))
    d_outer = d_second.astype(jnp.bfloat16)
    grad_bias_outer = jnp.sum(d_outer.astype(jnp.float32), axis=0)
    grad_outer = contract(gelu_low, d_outer, 0, 0)
    d_gelu = contract(d_outer, outer_full, 1, 1)
    (d_inner,) = gelu_back(d_gelu)
    d_inner_low = d_inner.astype(jnp.bfloat16)
    grad_bias_inner = jnp.sum(d_inner_low.astype(jnp.float32), axis=0)
    grad_inner = contract(first_low, d_inner_low, 0, 0)
    d_first = contract(d_inner_low, inner_full, 1, 1) + d_second
    d_resid, grad_gain_one, grad_bias_one = first_back(d_first)
    d_attn = d_resid.astype(jnp.bfloat16)
    grad_bias_output = jnp.sum(d_attn.astype(jnp.float32), axis=0)
    grad_output = contract(mixed_tok, d_attn, 1, 0)
    d_mixed = contract(output_full, d_attn, 1, 1).astype(jnp.bfloat16)
    d_mixed_flat = lax.all_to_all(d_mixed, "seq", split_axis=0, concat_axis=1, tiled=True)
    d_heads = d_mixed_flat.reshape(local_heads, head_size, stream_len)

    def backward_block(carry, block_index):
        d_keys, d_values = carry
        start_row = block_index * block_rows
        q_block, scores = block_scores(block_index)
        lse_block = lax.dynamic_slice_in_dim(log_sums, start_row, block_rows, 1)
        do_block = lax.dynamic_slice_in_dim(d_heads, start_row, block_rows, 2)
        probs = jnp.exp(scores - lse_block[..., None])
        d_probs = jnp.einsum("hdq,hdk->hqk", do_block, v_heads, preferred_element_type=jnp.float32)
        row_delta = jnp.sum(probs * d_probs, axis=-1, keepdims=True)
        d_scores = (probs * (d_probs - row_delta)).astype(jnp.bfloat16)
        d_query = (
            jnp.einsum("hqk,hdk->hdq", d_scores, k_heads, preferred_element_type=jnp.float32)
            * score_scale
        )
        d_keys = (
            d_keys
            + jnp.einsum("hqk,hdq->hdk", d_scores, q_block, preferred_element_type=jnp.float32)
            * score_scale
        )
        d_values = d_values + jnp.einsum(
            "hqk,hdq->hdk", probs.astype(jnp.bfloat16), do_block, preferred_element_type=jnp.float32
        )
        return ((d_keys, d_values), d_query)

    zero_heads = jnp.zeros((local_heads, head_size, stream_len), jnp.float32)
    (d_keys_all, d_values_all), d_query_blocks = lax.scan(
        backward_block, (zero_heads, zero_heads), jnp.arange(block_count)
    )
    d_query_flat = join_blocks(d_query_blocks).astype(jnp.bfloat16)
    d_key_flat = d_keys_all.reshape(local_heads * head_size, stream_len).astype(jnp.bfloat16)
    d_value_flat = d_values_all.reshape(local_heads * head_size, stream_len).astype(jnp.bfloat16)
    dq_tok, dk_tok, dv_tok = (
        lax.all_to_all(d_query_flat, "seq", split_axis=1, concat_axis=0, tiled=True),
        lax.all_to_all(d_key_flat, "seq", split_axis=1, concat_axis=0, tiled=True),
        lax.all_to_all(d_value_flat, "seq", split_axis=1, concat_axis=0, tiled=True),
    )
    grad_query = contract(tokens, dq_tok, 0, 1)
    grad_key = contract(tokens, dk_tok, 0, 1)
    grad_value = contract(tokens, dv_tok, 0, 1)
    grad_bias_query = jnp.sum(dq_tok.astype(jnp.float32), axis=1)
    grad_bias_value = jnp.sum(dv_tok.astype(jnp.float32), axis=1)
    d_tokens = (
        contract(dq_tok, query_full, 0, 1)
        + contract(dk_tok, key_full, 0, 1)
        + contract(dv_tok, value_full, 0, 1)
        + d_resid
    )
    grad_shards = (
        lax.psum_scatter(grad_query, "wshard", scatter_dimension=0, tiled=True),
        lax.psum_scatter(grad_key, "wshard", scatter_dimension=0, tiled=True),
        lax.psum_scatter(grad_value, "wshard", scatter_dimension=0, tiled=True),
        lax.psum_scatter(grad_output, "wshard", scatter_dimension=0, tiled=True),
        lax.psum_scatter(grad_inner, "wshard", scatter_dimension=0, tiled=True),
        lax.psum_scatter(grad_outer, "wshard", scatter_dimension=0, tiled=True),
        lax.psum_scatter(grad_bias_query, "wshard", scatter_dimension=0, tiled=True),
        lax.psum_scatter(grad_bias_value, "wshard", scatter_dimension=0, tiled=True),
        lax.psum_scatter(grad_bias_output, "wshard", scatter_dimension=0, tiled=True),
        lax.psum_scatter(grad_bias_inner, "wshard", scatter_dimension=0, tiled=True),
        lax.psum_scatter(grad_bias_outer, "wshard", scatter_dimension=0, tiled=True),
        lax.psum_scatter(grad_gain_one, "wshard", scatter_dimension=0, tiled=True),
        lax.psum_scatter(grad_bias_one, "wshard", scatter_dimension=0, tiled=True),
        lax.psum_scatter(grad_gain_two, "wshard", scatter_dimension=0, tiled=True),
        lax.psum_scatter(grad_bias_two, "wshard", scatter_dimension=0, tiled=True),
    )
    grad_total = (
        lax.psum(grad_shards[0].astype(jnp.bfloat16), "seq").astype(jnp.float32),
        lax.psum(grad_shards[1].astype(jnp.bfloat16), "seq").astype(jnp.float32),
        lax.psum(grad_shards[2].astype(jnp.bfloat16), "seq").astype(jnp.float32),
        lax.psum(grad_shards[3].astype(jnp.bfloat16), "seq").astype(jnp.float32),
        lax.psum(grad_shards[4].astype(jnp.bfloat16), "seq").astype(jnp.float32),
        lax.psum(grad_shards[5].astype(jnp.bfloat16), "seq").astype(jnp.float32),
        lax.psum(grad_shards[6].astype(jnp.bfloat16), "seq").astype(jnp.float32),
        lax.psum(grad_shards[7].astype(jnp.bfloat16), "seq").astype(jnp.float32),
        lax.psum(grad_shards[8].astype(jnp.bfloat16), "seq").astype(jnp.float32),
        lax.psum(grad_shards[9].astype(jnp.bfloat16), "seq").astype(jnp.float32),
        lax.psum(grad_shards[10].astype(jnp.bfloat16), "seq").astype(jnp.float32),
        lax.psum(grad_shards[11].astype(jnp.bfloat16), "seq").astype(jnp.float32),
        lax.psum(grad_shards[12].astype(jnp.bfloat16), "seq").astype(jnp.float32),
        lax.psum(grad_shards[13].astype(jnp.bfloat16), "seq").astype(jnp.float32),
        lax.psum(grad_shards[14].astype(jnp.bfloat16), "seq").astype(jnp.float32),
    )
    return (
        layer_output,
        d_tokens,
        grad_total[0],
        grad_total[1],
        grad_total[2],
        grad_total[3],
        grad_total[4],
        grad_total[5],
        grad_total[6],
        grad_total[7],
        grad_total[8],
        grad_total[9],
        grad_total[10],
        grad_total[11],
        grad_total[12],
        grad_total[13],
        grad_total[14],
    )


def solution(mesh):
    placed = (
        P(("wshard", "seq"), None),
        P(("wshard", "seq"), None),
        P("wshard", None),
        P("wshard", None),
        P("wshard", None),
        P("wshard", None),
        P("wshard", None),
        P("wshard", None),
        P("wshard", None),
        P("wshard"),
        P("wshard"),
        P("wshard"),
        P("wshard"),
        P("wshard"),
        P("wshard"),
        P("wshard"),
        P("wshard"),
        P("wshard"),
    )
    return jax.shard_map(
        shards,
        mesh=mesh,
        in_specs=placed,
        out_specs=(
            P(("wshard", "seq"), None),
            P(("wshard", "seq"), None),
            P("wshard", None),
            P("wshard", None),
            P("wshard", None),
            P("wshard", None),
            P("wshard", None),
            P("wshard", None),
            P("wshard"),
            P("wshard"),
            P("wshard"),
            P("wshard"),
            P("wshard"),
            P("wshard"),
            P("wshard"),
            P("wshard"),
            P("wshard"),
        ),
        check_vma=False,
    )
```

profile of v0, /device:TPU:0, one launch (start us, length us, event | category | flops | bytes accessed | tf_op | source)
XLA Modules:
  0.0 1432.2 jit_solution(7382742410380591382)
XLA Ops:
  19.3 39.9 %all-reduce.18 = (bf16[768]{0:T(1024)(128)(2,1)S(1)}, bf16[768]{0:T(1024)(128)(2,1)S(1)}, bf16[768]{0:T(1024)(128)(2,1)}, bf16[768]{0:T(1024)(128)(2,1)}, bf16[7...) all-reduce(bf16[768]{0:T(1024)(128)(2,1)S(1)} %dynamic-update-slice, ...), channel_id=1, replica_groups=mesh['wshard'=8,'seq'=4] {'wshard'}, use_global_device_ids=true, to_apply=%add | all-reduce | flops 6144 | bytes 24576
  66.6 29.6 %all-gather.8.cloned.1.call-done = bf16[768,768]{1,0:T(8,128)(2,1)} async-done(((bf16[96,768]{1,0:T(8,128)(2,1)}), bf16[768,768]{1,0:T(8,128)(2,1)}) %all-gather.8.cloned.1.call-update) | async-done | bytes 1179664 | tf_op jit(solution)/shard_map/all_gather | solution.py:58
  103.2 35.0 %all-gather.10.cloned.1.call-done = bf16[768,768]{1,0:T(8,128)(2,1)} async-done(((bf16[96,768]{1,0:T(8,128)(2,1)}), bf16[768,768]{1,0:T(8,128)(2,1)}) %all-gather.10.cloned.1.call-update) | async-done | bytes 1179664 | tf_op jit(solution)/shard_map/all_gather | solution.py:59
  164.9 127.5 %while.27 = (s32[]{:T(128)}, bf16[6,3,64,512]{3,2,1,0:T(8,128)(2,1)}, f32[6,3,512]{2,1,0:T(4,128)}, s32[6]{0:T(128)S(1)}, s32[3072]{0:T(1024)S(1)}, /*index=5*/b...) while((s32[]{:T(128)}, ...), condition=%wide.region_4.5_spmd, body=%wide.region_1.4_spmd.sunk | while | flops 1266153984 | bytes 65933512 | solution.py:129
  308.7 27.3 %all-gather = bf16[8,1,384]{2,1,0:T(2,128)(2,1)S(1)} all-gather(bf16[1,1,384]{2,1,0:T(2,128)(2,1)S(1)} %reshape.272), channel_id=1, replica_groups=mesh['wshard'=8,'seq'=4] {'wshard'}, dimensions={0}, use_global_device_ids=true | all-gather | bytes 6912 | tf_op jit(solution)/shard_map/all_gather | solution.py:67
  343.6 28.9 %multiply_convert_fusion.1 = (bf16[768,3072]{1,0:T(8,128)(2,1)}, f32[768,3072]{1,0:T(8,128)}, f32[768,3072]{1,0:T(8,128)}) fusion(f32[3072]{0:T(1024)} %bitcast.145, bf16[768,3072]{1,0:T(8,128)(2,1)} %all-gather.16.cloned.1.call-done, f32[768,768]{0,1:T(8,128)S(1)} %get-tuple-element.360, f32[768]{0:T(1024)} %convert_element_type.231, ...), kind=kOutput, calls=%fused_computation.45 | convolution fusion | flops 3782541312 | bytes 30695424 | tf_op jit(solution)/shard_map/dot_general | solution.py:137
  438.8 350.6 %while.28 = (s32[]{:T(128)}, f32[3,64,3072]{2,1,0:T(8,128)}, f32[3,64,3072]{2,1,0:T(8,128)}, bf16[6,3,64,512]{3,2,1,0:T(8,128)(2,1)}, s32[6]{0:T(128)S(1)}, /*in...) while((s32[]{:T(128)}, f32[3,64,3072]{2,1,0:T(8,128)}, ...), condition=%wide.region_15.16_spmd.clone, body=%wide.region_13.15_spmd.clone.sunk | while | flops 3095296512 | bytes 237564176 | solution.py:196
  460.1 14.4 %multiply_reduce_fusion.6 = (f32[3,512]{1,0:T(4,128)S(1)}, f32[3,512,3072]{2,1,0:T(8,128)}) fusion(f32[3,512,3072]{2,1,0:T(8,128)} %copy-done, f32[3,512]{1,0:T(4,128)S(1)} %constant_dynamic-slice_fusion.2, pred[512,3072]{1,0:T(8,128)(4,1)S(1)} %broadcast_compare_fusion.5, bf16[3,64,3072]{2,1,0:T(8,128)(2,1)} %get-tuple-element.565, ...), kind=kOutput, calls=%fused_computation.16.clone.1 | convolution fusion | flops 627571200 | bytes 40710148 | tf_op jit(solution)/shard_map/while/body/eval_jaxpr/hdq,hdk->hqk/dot_general | solution.py:178
  474.5 14.0 multiply_convert_fusion.3
  518.0 14.3 multiply_reduce_fusion.6
  532.3 13.9 multiply_convert_fusion.3
  576.6 14.3 multiply_reduce_fusion.6
  635.2 14.3 multiply_reduce_fusion.6
  649.5 13.9 multiply_convert_fusion.3
  693.8 14.3 multiply_reduce_fusion.6
  752.4 14.3 multiply_reduce_fusion.6
  792.6 18.4 %all_to_all.128 = bf16[192,4,768]{2,0,1:T(8,128)(2,1)S(1)} all-to-all(bf16[192,4,768]{2,0,1:T(8,128)(2,1)S(1)} %copy.148), channel_id=1, replica_groups=mesh['wshard'=8,'seq'=4] {'seq'}, dimensions={1} | all-to-all | bytes 2359296 | tf_op jit(solution)/shard_map/all_to_all | solution.py:203
  818.1 18.4 %all_to_all.129 = bf16[192,4,768]{2,0,1:T(8,128)(2,1)S(1)} all-to-all(bf16[192,4,768]{2,0,1:T(8,128)(2,1)S(1)} %copy.149), channel_id=1, replica_groups=mesh['wshard'=8,'seq'=4] {'seq'}, dimensions={1} | all-to-all | bytes 2359296 | tf_op jit(solution)/shard_map/all_to_all | solution.py:204
  843.5 18.4 %all_to_all.130 = bf16[192,4,768]{2,0,1:T(8,128)(2,1)S(1)} all-to-all(bf16[192,4,768]{2,0,1:T(8,128)(2,1)S(1)} %copy.152), channel_id=1, replica_groups=mesh['wshard'=8,'seq'=4] {'seq'}, dimensions={1} | all-to-all | bytes 2359296 | tf_op jit(solution)/shard_map/all_to_all | solution.py:205
  898.8 54.9 %reduce-scatter.21.cloned.1.call-done = f32[96,768]{1,0:T(8,128)} async-done(((f32[768,768]{1,0:T(8,128)}), f32[96,768]{1,0:T(8,128)}) %reduce-scatter.21.cloned.1.call-update) | async-done | bytes 294928
  955.5 70.4 %reduce-scatter.23.cloned.1.call-done = f32[96,768]{1,0:T(8,128)} async-done(((f32[768,768]{1,0:T(8,128)}), f32[96,768]{1,0:T(8,128)}) %reduce-scatter.23.cloned.1.call-update) | async-done | bytes 294928
  1027.7 163.2 %reduce-scatter.15.cloned.1.call-done = f32[96,3072]{1,0:T(8,128)} async-done(((f32[768,3072]{1,0:T(8,128)}), f32[96,3072]{1,0:T(8,128)}) %reduce-scatter.15.cloned.1.call-update) | async-done | bytes 1179664 | tf_op jit(solution)/shard_map/reduce_scatter | solution.py:223
  1193.1 162.5 %reduce-scatter.17.cloned.1.call-done = f32[384,768]{1,0:T(8,128)} async-done(((f32[3072,768]{1,0:T(8,128)}), f32[384,768]{1,0:T(8,128)}) %reduce-scatter.17.cloned.1.call-update) | async-done | bytes 1179664 | tf_op jit(solution)/shard_map/reduce_scatter | solution.py:224
  1368.1 35.9 %all-reduce.17 = (bf16[768]{0:T(1024)(128)(2,1)S(1)}, bf16[768]{0:T(1024)(128)(2,1)S(1)}, bf16[768]{0:T(1024)(128)(2,1)S(1)}, bf16[3072]{0:T(1024)(128)(2,1)S(1)...) all-reduce(f32[768]{0:T(1024)S(1)} %reduce_sum.226, ...), channel_id=8, replica_groups=mesh['wshard'=8,'seq'=4] {'wshard'}, use_global_device_ids=true, to_apply=%region_29.30.clone | all-reduce | flops 9216 | bytes 55296
  (376 shorter events, 576.0 us)
Async XLA Ops:
  7.2 52.0 %all-gather.12.cloned.1.call-start = ((), (), s32[]{:S(2)}) async-start(), calls=%async_computation.16 | async-start | bytes 1327104 | tf_op jit(solution)/shard_map/all_gather | solution.py:60
  7.9 88.3 %all-gather.8.cloned.1.call-start = ((), (), s32[]{:S(2)}) async-start(), calls=%async_computation.14 | async-start | bytes 1327104 | tf_op jit(solution)/shard_map/all_gather | solution.py:58
  8.7 129.5 %all-gather.10.cloned.1.call-start = ((), (), s32[]{:S(2)}) async-start(), calls=%async_computation.15 | async-start | bytes 1327104 | tf_op jit(solution)/shard_map/all_gather | solution.py:59
  9.4 327.9 %all-gather.14.cloned.1.call-start = ((), (), s32[]{:S(2)}) async-start(), calls=%async_computation.17 | async-start | bytes 1327104 | tf_op jit(solution)/shard_map/all_gather | solution.py:61
  10.0 333.6 %all-gather.16.cloned.1.call-start = ((), (), s32[]{:S(2)}) async-start(), calls=%async_computation.18 | async-start | bytes 5308416 | tf_op jit(solution)/shard_map/all_gather | solution.py:62
  63.0 33.3 %copy-start.13 = (bf16[768,768]{1,0:T(8,128)(2,1)S(1)}, bf16[768,768]{1,0:T(8,128)(2,1)}, u32[]{:S(2)}) copy-start(bf16[768,768]{1,0:T(8,128)(2,1)} %param.22) | copy-start | bytes 3538948
  63.0 36.7 %all-to-all-start.2 = ((bf16[4,192,768]{2,1,0:T(8,128)(2,1)}), bf16[4,192,768]{2,1,0:T(8,128)(2,1)S(1)}, u32[]{:S(2)}, u32[]{:S(2)}) async-start(bf16[4,192,768]{2,1,0:T(8,128)(2,1)} %bitcast.10), calls=%async_computation.2 | async-start | bytes 2359296 | tf_op jit(solution)/shard_map/all_to_all | solution.py:96
  99.7 42.0 %all-to-all-start = ((bf16[4,192,768]{2,1,0:T(8,128)(2,1)}), bf16[4,192,768]{2,1,0:T(8,128)(2,1)S(1)}, u32[]{:S(2)}, u32[]{:S(2)}) async-start(bf16[4,192,768]{2,1,0:T(8,128)(2,1)} %bitcast.143), calls=%async_computation | async-start | bytes 2359296 | tf_op jit(solution)/shard_map/all_to_all | solution.py:94
  141.6 19.5 %all-to-all-start.1 = ((bf16[4,192,768]{2,1,0:T(8,128)(2,1)}), bf16[4,192,768]{2,1,0:T(8,128)(2,1)S(1)}, u32[]{:S(2)}, u32[]{:S(2)}) async-start(bf16[4,192,768]{2,1,0:T(8,128)(2,1)} %bitcast.141), calls=%async_computation.1 | async-start | bytes 2359296 | tf_op jit(solution)/shard_map/all_to_all | solution.py:95
  145.3 227.3 %all-gather.18.cloned.1.call-start = ((), (), s32[]{:S(2)}) async-start(), calls=%async_computation.19 | async-start | bytes 5308416 | tf_op jit(solution)/shard_map/all_gather | solution.py:63
  296.5 40.1 %copy-start.12 = (bf16[768,768]{1,0:T(8,128)(2,1)S(1)}, bf16[768,768]{1,0:T(8,128)(2,1)}, u32[]{:S(2)}) copy-start(bf16[768,768]{1,0:T(8,128)(2,1)} %param.23) | copy-start | bytes 3538948
  296.5 40.7 %all-to-all-start.3 = ((bf16[192,4,768]{2,0,1:T(8,128)(2,1)}), bf16[192,4,768]{2,0,1:T(8,128)(2,1)S(1)}, u32[]{:S(2)}, u32[]{:S(2)}) async-start(bf16[192,4,768]{2,0,1:T(8,128)(2,1)} %copy.143), calls=%async_computation.3 | async-start | bytes 2359296 | tf_op jit(solution)/shard_map/all_to_all | solution.py:132
  341.5 66.4 %copy-start.4 = (f32[768,768]{0,1:T(8,128)}, f32[768,768]{0,1:T(8,128)S(1)}, u32[]{:S(2)}) copy-start(f32[768,768]{0,1:T(8,128)S(1)} %get-tuple-element.360) | copy-start | bytes 7077892
  412.8 19.5 %all-to-all-start.4 = ((bf16[4,192,768]{2,1,0:T(8,128)(2,1)}), bf16[4,192,768]{2,1,0:T(8,128)(2,1)S(1)}, u32[]{:S(2)}, u32[]{:S(2)}) async-start(bf16[4,192,768]{2,1,0:T(8,128)(2,1)} %bitcast.142), calls=%async_computation.4 | async-start | bytes 2359296 | tf_op jit(solution)/shard_map/all_to_all | solution.py:168
  416.5 478.9 %reduce-scatter.13.cloned.1.call-start = ((), (), s32[]{:S(2)}) async-start(), calls=%async_computation.20 | async-start | bytes 2654208 | tf_op jit(solution)/shard_map/reduce_scatter | solution.py:222
  419.2 477.9 %reduce-scatter.19.cloned.1.call-start = ((), (), s32[]{:S(2)}) async-start(), calls=%async_computation.23 | async-start | bytes 2654208
  792.5 19.6 %copy-start.15 = (bf16[768,768]{1,0:T(8,128)(2,1)S(1)}, bf16[768,768]{1,0:T(8,128)(2,1)}, u32[]{:S(2)}) copy-start(bf16[768,768]{1,0:T(8,128)(2,1)} %param.22) | copy-start | bytes 3538948
  815.1 138.7 %reduce-scatter.21.cloned.1.call-start = ((), (), s32[]{:S(2)}) async-start(), calls=%async_computation.24 | async-start | bytes 2654208
  840.6 185.4 %reduce-scatter.23.cloned.1.call-start = ((), (), s32[]{:S(2)}) async-start(), calls=%async_computation.25 | async-start | bytes 2654208
  865.1 325.9 %reduce-scatter.15.cloned.1.call-start = ((), (), s32[]{:S(2)}) async-start(), calls=%async_computation.21 | async-start | bytes 10616832 | tf_op jit(solution)/shard_map/reduce_scatter | solution.py:223
  875.7 479.9 %reduce-scatter.17.cloned.1.call-start = ((), (), s32[]{:S(2)}) async-start(), calls=%async_computation.22 | async-start | bytes 10616832 | tf_op jit(solution)/shard_map/reduce_scatter | solution.py:224
  885.9 529.3 %all-reduce.23.cloned.1.call-start = ((), (), s32[]{:S(2)}) async-start(), calls=%async_computation.26 | async-start | bytes 3833856 | tf_op jit(solution)/shard_map/psum | solution.py:236
  1193.1 166.3 %copy-start.3 = (f32[768,768]{0,1:T(8,128)S(1)}, f32[768,768]{0,1:T(8,128)}, u32[]{:S(2)}) copy-start(f32[768,768]{0,1:T(8,128)} %copy-done.2) | copy-start | bytes 7077892
  1193.1 166.3 %copy-start.24 = (f32[768]{0:T(1024)S(1)}, f32[768]{0:T(1024)}, u32[]{:S(2)}) copy-start(f32[768]{0:T(1024)} %copy-done.23) | copy-start | bytes 9220
  (50 other events, 271.6 us)
Sparse Core Ops, SparseCore 0:
  10.2 44.0 all-gather.11
  56.4 39.7 all-gather.7
  98.4 39.7 all-gather.9
  140.3 39.7 all-gather.13
  182.1 78.0 all-gather.15
  262.2 77.7 all-gather.17
  420.8 67.4 reduce-scatter.12
  815.2 66.1 reduce-scatter.18
  884.9 68.8 reduce-scatter.20
  957.1 68.8 reduce-scatter.22
  1029.6 161.3 reduce-scatter.14
  1194.4 161.1 reduce-scatter.16
  1359.0 47.7 all-reduce.22
where the time goes:
time: 1440 us; the launch traced here: 1430 us
  waiting for transfers between devices  540 us (38%)
  matrix products  398 us (28%)
  blocking collectives  164 us (11%)
  other arithmetic  164 us (11%)
  local copies, waits for them, and re-layouts  122 us (8%)
  starting transfers between devices  18.7 us (1%)
  between operations  16.9 us (1%)
    reduce_scatter x1, waiting for transfers between devices, shards(): lax.psum_scatter(grad_inner, 'wshard', scatter_dimension=0, tiled=True)  163 us
    reduce_scatter x1, waiting for transfers between devices, shards(): lax.psum_scatter(grad_outer, 'wshard', scatter_dimension=0, tiled=True)  163 us
    unnamed x16, waiting for transfers between devices  129 us
    dot_general x6, matrix products, backward_block(): jnp.einsum('hdq,hdk->hqk', do_block, v_heads, preferred_element_type=jnp....  85.9 us
    convert_element_type x6, other arithmetic, backward_block(): d_scores = (probs * (d_probs - row_delta)).astype(jnp.bfloat16)  83.3 us
    unnamed x2, blocking collectives  75.9 us
    dot_general x16, matrix products, contract(): lax.dot_general(left_in, right_in, (((left_dim,), (right_dim,)), ((), ())...  72.4 us
    dot_general x12, matrix products, block_scores(): jnp.einsum('hdq,hdk->hqk', q_block, k_heads, preferred_element_type=jnp.f...  53.4 us
  transfers between devices with their start and end apart: 18, of which 8 were waited for; matrix products, arithmetic and copies ran while one was open for 41% of the time, Pallas kernels for 0%

commit v1 on v0

v1 whole, which is shorter than its diff:
```python
import functools

import jax
import jax.numpy as jnp
from jax import lax
from jax.experimental import pallas as pl
from jax.experimental.pallas import tpu as pltpu
from jax.sharding import PartitionSpec as P

NORM_EPS = 1e-05

HD = 64
bf = jnp.bfloat16
f32 = jnp.float32

def doc_bounds(starts_ref, pos, total):
    lo = jnp.zeros_like(pos); hi = jnp.full_like(pos, total)
    for d in range(starts_ref.shape[1]):
        s = starts_ref[0, d]
        lo = jnp.where(s <= pos, jnp.maximum(lo, s), lo)
        hi = jnp.where(s > pos, jnp.minimum(hi, s), hi)
    return lo, hi

def dot(a, b):
    return lax.dot_general(a, b, (((1,), (0,)), ((), ())), preferred_element_type=f32)

def fwd_kernel(heads, bq, bk, starts, qT, k3, vT, oT, mixT, lse, acc, ml):
    total = k3.shape[1]
    i = pl.program_id(0)
    q0 = i * bq
    first, _ = doc_bounds(starts, jnp.int32(q0), total)
    _, last = doc_bounds(starts, jnp.int32(q0 + bq - 1), total)
    pos = q0 + lax.broadcasted_iota(jnp.int32, (1, bq), 1)
    lo, hi = doc_bounds(starts, pos, total)
    kb0 = first // bk
    kb1 = (last + bk - 1) // bk
    acc[...] = jnp.zeros_like(acc)
    ml[0] = jnp.full((heads, bq), -1e30, f32)
    ml[1] = jnp.zeros((heads, bq), f32)
    kio = lax.broadcasted_iota(jnp.int32, (bk, bq), 0)
    def body(j, _):
        ks = pl.multiple_of(j * bk, bk)
        mask = (kio >= lo - ks) & (kio < hi - ks)
        for h in range(heads):
            s = dot(k3[h, pl.ds(ks, bk), :], qT[HD * h:HD * (h + 1), :])
            s = jnp.where(mask, s, -1e30)
            m_old = ml[0, h:h + 1]
            m = jnp.maximum(m_old, jnp.max(s, axis=0, keepdims=True))
            p = jnp.exp(s - m)
            al = jnp.exp(m_old - m)
            ml[0, h:h + 1] = m
            ml[1, h:h + 1] = ml[1, h:h + 1] * al + jnp.sum(p, axis=0, keepdims=True)
            sl = slice(HD * h, HD * (h + 1))
            acc[sl, :] = acc[sl, :] * al + dot(vT[sl, pl.ds(ks, bk)], p.astype(bf))
        return 0
    lax.fori_loop(kb0, kb1, body, 0)
    for h in range(heads):
        sl = slice(HD * h, HD * (h + 1))
        l = ml[1, h:h + 1]
        o = acc[sl, :] / l
        oT[sl, :] = o
        mixT[sl, :] = o.astype(bf)
        lse[h:h + 1, :] = ml[0, h:h + 1] + jnp.log(l)

def attn_fwd(starts, qT, k3, vT, bq=256, bk=256):
    heads, total, _ = k3.shape
    full2 = lambda i: (0, 0)
    return pl.pallas_call(
        functools.partial(fwd_kernel, heads, bq, bk),
        grid=(total // bq,),
        in_specs=[pl.BlockSpec(memory_space=pltpu.SMEM),
                  pl.BlockSpec((heads * HD, bq), lambda i: (0, i)),
                  pl.BlockSpec(k3.shape, lambda i: (0, 0, 0)),
                  pl.BlockSpec(vT.shape, full2)],
        out_specs=[pl.BlockSpec((heads * HD, bq), lambda i: (0, i)),
                   pl.BlockSpec((heads * HD, bq), lambda i: (0, i)),
                   pl.BlockSpec((heads, bq), lambda i: (0, i))],
        out_shape=[jax.ShapeDtypeStruct((heads * HD, total), f32),
                   jax.ShapeDtypeStruct((heads * HD, total), bf),
                   jax.ShapeDtypeStruct((heads, total), f32)],
        scratch_shapes=[pltpu.VMEM((heads * HD, bq), f32), pltpu.VMEM((2, heads, bq), f32)],
        name="attn_fwd",
    )(starts, qT, k3, vT)

def bwd_kernel(heads, bq, bk, starts, qT, q3, k3, kT, v3, doT, do3, oT, lse, dqT, dk3, dv3, delta, dqa, dka, dva):
    total = q3.shape[1]
    i = pl.program_id(0)
    k0 = i * bk
    @pl.when(i == 0)
    def _():
        dqa[...] = jnp.zeros_like(dqa)
        for h in range(heads):
            sl = slice(HD * h, HD * (h + 1))
            delta[h:h + 1, :] = jnp.sum(doT[sl, :].astype(f32) * oT[sl, :], axis=0, keepdims=True)
    first, _ = doc_bounds(starts, jnp.int32(k0), total)
    _, last = doc_bounds(starts, jnp.int32(k0 + bk - 1), total)
    qb0 = first // bq
    qb1 = (last + bq - 1) // bq
    dka[...] = jnp.zeros_like(dka)
    dva[...] = jnp.zeros_like(dva)
    kio = k0 + lax.broadcasted_iota(jnp.int32, (bk, bq), 0)
    def body(j, _):
        qs = pl.multiple_of(j * bq, bq)
        pos = qs + lax.broadcasted_iota(jnp.int32, (1, bq), 1)
        lo, hi = doc_bounds(starts, pos, total)
        mask = (kio >= lo) & (kio < hi)
        for h in range(heads):
            sl = slice(HD * h, HD * (h + 1))
            s = dot(k3[h, :, :], qT[sl, pl.ds(qs, bq)])
            p = jnp.exp(jnp.where(mask, s - lse[h:h + 1, pl.ds(qs, bq)], -1e30))
            dp = dot(v3[h, :, :], doT[sl, pl.ds(qs, bq)])
            ds = p * (dp - delta[h:h + 1, pl.ds(qs, bq)])
            dsb = ds.astype(bf)
            dva[h] += dot(p.astype(bf), do3[h, pl.ds(qs, bq), :])
            dka[h] += dot(dsb, q3[h, pl.ds(qs, bq), :])
            dqa[sl, pl.ds(qs, bq)] += dot(kT[sl, :], dsb)
        return 0
    lax.fori_loop(qb0, qb1, body, 0)
    dk3[...] = dka[...].astype(bf)
    dv3[...] = dva[...].astype(bf)
    @pl.when(i == pl.num_programs(0) - 1)
    def _():
        dqT[...] = (dqa[...] * (HD ** -0.5)).astype(bf)

def attn_bwd(starts, qT, q3, k3, kT, v3, doT, do3, oT, lse, bq=256, bk=256):
    heads, total, _ = k3.shape
    full = lambda a: pl.BlockSpec(a.shape, lambda i: (0,) * a.ndim)
    kb3 = pl.BlockSpec((heads, bk, HD), lambda i: (0, i, 0))
    return pl.pallas_call(
        functools.partial(bwd_kernel, heads, bq, bk),
        grid=(total // bk,),
        in_specs=[pl.BlockSpec(memory_space=pltpu.SMEM), full(qT), full(q3), kb3,
                  pl.BlockSpec((heads * HD, bk), lambda i: (0, i)), kb3, full(doT), full(do3), full(oT), full(lse)],
        out_specs=[full(qT), kb3, kb3],
        out_shape=[jax.ShapeDtypeStruct(qT.shape, bf), jax.ShapeDtypeStruct(k3.shape, bf), jax.ShapeDtypeStruct(k3.shape, bf)],
        scratch_shapes=[pltpu.VMEM((heads, total), f32), pltpu.VMEM(qT.shape, f32),
                        pltpu.VMEM((heads, bk, HD), f32), pltpu.VMEM((heads, bk, HD), f32)],
        name="attn_bwd",
    )(starts, qT, q3, k3, kT, v3, doT, do3, oT, lse)


def layer_norm(inputs, norm_gain, norm_bias):
    row_mean = jnp.mean(inputs, axis=-1, keepdims=True)
    centred = inputs - row_mean
    row_var = jnp.mean(centred * centred, axis=-1, keepdims=True)
    return centred * lax.rsqrt(row_var + NORM_EPS) * norm_gain + norm_bias


def gelu_exact(inputs):
    return jax.nn.gelu(inputs, approximate=False)


def contract(left_in, right_in, left_dim, right_dim):
    return lax.dot_general(
        left_in,
        right_in,
        (((left_dim,), (right_dim,)), ((), ())),
        preferred_element_type=jnp.float32,
    )


def shards(
    tokens, cotangent, starts,
    w_query, w_key, w_value, w_output, w_inner, w_outer,
    b_query, b_value, b_output, b_inner, b_outer,
    gain_first, bias_first, gain_second, bias_second,
):
    model = tokens.shape[1]
    seq_n = lax.axis_size("seq")
    seq_i = lax.axis_index("seq")
    shard_i = lax.axis_index("wshard")
    width = model // seq_n
    heads = width // HD

    def own(columns):
        return lax.dynamic_slice_in_dim(columns, seq_i * width, width, columns.ndim - 1)

    def gather(shard):
        return lax.all_gather(shard, "wshard", axis=0, tiled=True)

    smalls = (b_query, b_value, b_output, b_inner, b_outer, gain_first, bias_first, gain_second, bias_second)
    sizes = [member.shape[0] for member in smalls]
    packed = lax.all_gather(jnp.concatenate(smalls), "wshard", axis=0, tiled=False).astype(f32)
    full, at = [], 0
    for size in sizes:
        full.append(packed[:, at:at + size].reshape(-1))
        at += size
    bias_query, bias_value, bias_output, bias_inner, bias_outer, gain_one, shift_one, gain_two, shift_two = full

    stream = lax.all_gather(tokens, "seq", axis=0, tiled=True)
    w_own = gather(jnp.concatenate([own(w_query), own(w_key), own(w_value)], axis=1))
    output_full, inner_full, outer_full = gather(w_output), gather(w_inner), gather(w_outer)
    scale = HD ** -0.5
    qT = ((contract(w_own[:, :width], stream, 0, 1) + own(bias_query)[:, None]).astype(bf) * bf(scale))
    kT = contract(w_own[:, width:2 * width], stream, 0, 1).astype(bf)
    vT = (contract(w_own[:, 2 * width:], stream, 0, 1) + own(bias_value)[:, None]).astype(bf)

    def by_token(arr):
        return arr.reshape(heads, HD, -1).transpose(0, 2, 1)

    def by_feature(arr):
        return arr.transpose(0, 2, 1).reshape(width, -1)

    q3, k3, v3 = by_token(qT), by_token(kT), by_token(vT)
    oT, mixT, lse = attn_fwd(starts, qT, k3, vT, 512, 512)
    mixed = lax.all_to_all(mixT, "seq", split_axis=1, concat_axis=0, tiled=True)

    residual_in = tokens.astype(f32) + contract(mixed, output_full, 0, 0) + bias_output
    first_norm, first_back = jax.vjp(layer_norm, residual_in, gain_one, shift_one)
    first_low = first_norm.astype(bf)
    inner_act = jnp.dot(first_low, inner_full, preferred_element_type=f32) + bias_inner
    gelu_out, gelu_back = jax.vjp(gelu_exact, inner_act)
    gelu_low = gelu_out.astype(bf)
    second_in = first_norm + jnp.dot(gelu_low, outer_full, preferred_element_type=f32) + bias_outer
    layer_result, second_back = jax.vjp(layer_norm, second_in, gain_two, shift_two)
    d_second, grad_gain_two, grad_bias_two = second_back(cotangent.astype(f32))
    d_outer = d_second.astype(bf)
    grad_bias_outer = jnp.sum(d_outer.astype(f32), axis=0)
    grad_outer = contract(gelu_low, d_outer, 0, 0)
    (d_inner,) = gelu_back(contract(d_outer, outer_full, 1, 1))
    d_inner_low = d_inner.astype(bf)
    grad_bias_inner = jnp.sum(d_inner_low.astype(f32), axis=0)
    grad_inner = contract(first_low, d_inner_low, 0, 0)
    d_first = contract(d_inner_low, inner_full, 1, 1) + d_second
    d_resid, grad_gain_one, grad_bias_one = first_back(d_first)
    d_attn = d_resid.astype(bf)
    grad_bias_output = jnp.sum(d_attn.astype(f32), axis=0)
    grad_output = contract(mixed, d_attn, 1, 0)
    d_mixed = contract(output_full, d_attn, 1, 1).astype(bf)
    doT = lax.all_to_all(d_mixed, "seq", split_axis=0, concat_axis=1, tiled=True)

    dqT, dk3, dv3 = attn_bwd(starts, qT, q3, k3, kT, v3, doT, by_token(doT), oT, lse, 256, 512)
    dT = jnp.concatenate([dqT, by_feature(dk3), by_feature(dv3)], axis=0)
    grad_own = contract(stream, dT, 0, 1).astype(bf)
    d_part = contract(dT, w_own, 0, 1).astype(bf)
    d_tokens = lax.psum_scatter(d_part, "seq", scatter_dimension=0, tiled=True).astype(f32) + d_resid

    def spread(own_sum):
        return lax.dynamic_update_slice(jnp.zeros((model,), f32), own_sum, (seq_i * width,))

    grad_small = (
        spread(jnp.sum(dqT.astype(f32), axis=1)),
        spread(jnp.sum(dv3.astype(f32), axis=1).reshape(-1)),
        grad_bias_output, grad_bias_inner, grad_bias_outer,
        grad_gain_one, grad_bias_one, grad_gain_two, grad_bias_two,
    )
    shards_n = lax.axis_size("wshard")
    small_sum = lax.psum(
        jnp.concatenate([member.reshape(shards_n, -1) for member in grad_small], axis=1), ("wshard", "seq")
    )
    small_own = lax.dynamic_index_in_dim(small_sum, shard_i, 0, keepdims=False)
    outs, at = [], 0
    for size in sizes:
        outs.append(small_own[at:at + size])
        at += size

    def scatter(grad):
        low = lax.psum_scatter(grad.astype(bf), "wshard", scatter_dimension=0, tiled=True)
        return lax.psum(low, "seq").astype(f32)

    own_shard = lax.psum_scatter(grad_own, "wshard", scatter_dimension=0, tiled=True)
    parts = lax.all_gather(own_shard, "seq", axis=0, tiled=False).astype(f32)
    qkv_grads = [
        parts[:, :, i * width:(i + 1) * width].transpose(1, 0, 2).reshape(-1, model) for i in range(3)
    ]
    return (
        layer_result.astype(bf), d_tokens, *qkv_grads,
        scatter(grad_output), scatter(grad_inner), scatter(grad_outer), *outs,
    )


def solution(mesh):
    placed = (
        P(("wshard", "seq"), None),
        P(("wshard", "seq"), None),
        P("wshard", None),
        P("wshard", None),
        P("wshard", None),
        P("wshard", None),
        P("wshard", None),
        P("wshard", None),
        P("wshard", None),
        P("wshard"),
        P("wshard"),
        P("wshard"),
        P("wshard"),
        P("wshard"),
        P("wshard"),
        P("wshard"),
        P("wshard"),
        P("wshard"),
    )
    return jax.shard_map(
        shards,
        mesh=mesh,
        in_specs=placed,
        out_specs=(
            P(("wshard", "seq"), None),
            P(("wshard", "seq"), None),
            P("wshard", None),
            P("wshard", None),
            P("wshard", None),
            P("wshard", None),
            P("wshard", None),
            P("wshard", None),
            P("wshard"),
            P("wshard"),
            P("wshard"),
            P("wshard"),
            P("wshard"),
            P("wshard"),
            P("wshard"),
            P("wshard"),
            P("wshard"),
        ),
        check_vma=False,
    )
```

time: 1440 us -> 732 us (0.51)
  matrix products: 398 us -> 112 us
  waiting for transfers between devices: 540 us -> 320 us
  other arithmetic: 164 us -> 17.5 us
  Pallas kernels: 0 us -> 80.6 us
  local copies, waits for them, and re-layouts: 122 us -> 57 us
  blocking collectives: 164 us -> 113 us
    dot_general x44 -> x2, matrix products: 326 us -> 38.6 us  [the longest x1 29.7 us: shards(): jnp.dot(first_low, inner_full, preferred_element_type=f32) + bias_inner]
    unnamed x16 -> x10, waiting for transfers between devices: 129 us -> 2.68 us
    reduce_scatter x3 -> x5, waiting for transfers between devices: 326 us -> 204 us  [the longest x3 148 us: scatter(): lax.psum_scatter(grad.astype(bf), 'wshard', scatter_dimension=0, tiled=True)]
    convert_element_type x32 -> x4, other arithmetic: 108 us -> 5.17 us  [the longest x3 5.1 us: scatter(): return lax.psum(low, 'seq').astype(f32)]
    pallas_call x0 -> x2, Pallas kernels: none -> 80.6 us  [the longest x1 40.5 us: attn_bwd(): pl.pallas_call(functools.partial(bwd_kernel, heads, bq, bk), grid=(total...]
    unnamed x2 -> x0, blocking collectives: 75.9 us -> none
    all_to_all x3 -> x0, blocking collectives: 55.2 us -> none  [the longest x1 18.4 us: shards(): lax.all_to_all(d_query_flat, 'seq', split_axis=1, concat_axis=0, tiled=True)]
    all_gather x1 -> x3, blocking collectives: 27.3 us -> 72.9 us  [the longest x1 34.6 us: gather(): return lax.all_gather(shard, 'wshard', axis=0, tiled=True)]
  transfers between devices with their start and end apart: 18 -> 12, of which waited for: 8 -> 9; matrix products, arithmetic and copies ran while one was open for 41% -> 19% of each run, Pallas kernels for 0% -> 11%
where the time goes in v1:
time: 732 us; the launch traced here: 725 us
  waiting for transfers between devices  320 us (44%)
  blocking collectives  113 us (15%)
  matrix products  112 us (15%)
  Pallas kernels  80.6 us (11%)
  local copies, waits for them, and re-layouts  57 us (8%)
  other arithmetic  17.5 us (2%)
  between operations  14.9 us (2%)
  starting transfers between devices  9.77 us (1%)
    reduce_scatter x3, waiting for transfers between devices, scatter(): lax.psum_scatter(grad.astype(bf), 'wshard', scatter_dimension=0, tiled=True)  148 us
    dot_general x12, matrix products, contract(): lax.dot_general(left_in, right_in, (((left_dim,), (right_dim,)), ((), ())...  73.5 us
    all_gather x3, waiting for transfers between devices, gather(): return lax.all_gather(shard, 'wshard', axis=0, tiled=True)  65.8 us
    reduce_scatter x1, waiting for transfers between devices, shards(): lax.psum_scatter(d_part, 'seq', scatter_dimension=0, tiled=True).astype(f32)  45.1 us
    psum x1, blocking collectives, shards(): lax.psum(jnp.concatenate([member.reshape(shards_n, -1) for member in grad...  40.6 us
    pallas_call x1, Pallas kernels, attn_bwd(): pl.pallas_call(functools.partial(bwd_kernel, heads, bq, bk), grid=(total...  40.5 us
    pallas_call x1, Pallas kernels, attn_fwd(): pl.pallas_call(functools.partial(fwd_kernel, heads, bq, bk), grid=(total...  40.1 us
    all_gather x1, blocking collectives, gather(): return lax.all_gather(shard, 'wshard', axis=0, tiled=True)  34.6 us
  transfers between devices with their start and end apart: 12, of which 9 were waited for; matrix products, arithmetic and copies ran while one was open for 19% of the time, Pallas kernels for 11%

profile of v1, /device:TPU:0, one launch (start us, length us, event | category | flops | bytes accessed | tf_op | source)
XLA Modules:
  0.0 725.1 jit_solution(13181815688915424994)
XLA Ops:
  11.3 34.6 %all_gather.27 = bf16[768,576]{1,0:T(8,128)(2,1)S(1)} all-gather(bf16[96,576]{1,0:T(8,128)(2,1)S(1)} %pad_maximum_fusion.7), channel_id=1, replica_groups=mesh['wshard'=8,'seq'=4] {'wshard'}, dimensions={0}, use_global_device_ids=true | all-gather | bytes 995328 | tf_op jit(solution)/shard_map/all_gather | solution.py:179
  46.1 30.9 %all-gather.2 = bf16[8,1,1152]{2,1,0:T(2,128)(2,1)S(1)} all-gather(bf16[1,1,1152]{2,1,0:T(2,128)(2,1)S(1)} %reshape.211), channel_id=2, replica_groups=mesh['wshard'=8,'seq'=4] {'wshard'}, dimensions={0}, use_global_device_ids=true | all-gather | bytes 20736 | tf_op jit(solution)/shard_map/all_gather | solution.py:183
  77.4 5.3 fusion.8.qT
  89.9 40.1 %attn_fwd.1 = (f32[192,3072]{1,0:T(8,128)}, bf16[192,3072]{1,0:T(8,128)(2,1)}, f32[3,3072]{1,0:T(4,128)}) custom-call(s32[1,8]{1,0:T(1,128)} %starts.3, bf16[192,3072]{1,0:T(8,128)(2,1)} %fusion.8.qT, bf16[3,3072,64]{2,1,0:T(8,128)(2,1)} %bitcast.75, bf16[192,3072]{1,0:T(8,128)(2,1)} %fusion.7.vT), custom_call_target="tpu_custom_call" | custom-call | tf_op jit(solution)/shard_map/attn_fwd/pallas_call | solution.py:68
  140.2 12.7 %all-to-all-done = bf16[192,4,768]{2,0,1:T(8,128)(2,1)} async-done(((bf16[192,4,768]{2,0,1:T(8,128)(2,1)}), bf16[192,4,768]{2,0,1:T(8,128)(2,1)}, u32[]{:S(2)}, u32[]{:S(2)}) %all-to-all-start) | async-done | bytes 1179680 | tf_op jit(solution)/shard_map/all_to_all | solution.py:206
  157.8 15.7 %all-gather.12.cloned.1.call-done = bf16[768,3072]{1,0:T(8,128)(2,1)} async-done(((bf16[96,3072]{1,0:T(8,128)(2,1)}), bf16[768,3072]{1,0:T(8,128)(2,1)}) %all-gather.12.cloned.1.call-update) | async-done | bytes 4718608 | tf_op jit(solution)/shard_map/all_gather | solution.py:179
  173.5 29.7 %multiply_convert_fusion = (bf16[768,3072]{1,0:T(8,128)(2,1)}, f32[768,3072]{1,0:T(8,128)}, f32[768,3072]{1,0:T(8,128)}) fusion(f32[3072]{0:T(1024)S(1)} %add.142, bf16[768,3072]{1,0:T(8,128)(2,1)} %all-gather.12.cloned.1.call-done, f32[768,768]{0,1:T(8,128)} %copy-done.2, f32[768]{0:T(1024)S(1)} %add.139, f32[768]{0:T(1024)S(1)} %mul.161, ...), kind=kOutput, calls=%fused_computation.4 | convolution fusion | flops 3782541312 | bytes 30695424 | tf_op jit(solution)/shard_map/dot_general | solution.py:211
  203.2 50.1 %all-gather.14.cloned.1.call-done = bf16[3072,768]{1,0:T(8,128)(2,1)} async-done(((bf16[384,768]{1,0:T(8,128)(2,1)}), bf16[3072,768]{1,0:T(8,128)(2,1)}) %all-gather.14.cloned.1.call-update) | async-done | bytes 4718608 | tf_op jit(solution)/shard_map/all_gather | solution.py:179
  253.3 9.0 %fusion.33 = (f32[768]{0:T(1024)S(1)}, f32[768,768]{0,1:T(8,128)S(1)}) fusion(f32[768]{0:T(1024)S(1)} %add.146, bf16[768,3072]{1,0:T(8,128)(2,1)} %get-tuple-element.116, bf16[3072,768]{1,0:T(8,128)(2,1)} %all-gather.14.cloned.1.call-done, f32[768]{0:T(1024)S(1)} %add.139, f32[768]{0:T(1024)S(1)} %mul.161, f32[768]{0:T(1024)S(1)} %fusion.20, ...), kind=kOutput, calls=%fused_computation.98 | convolution fusion | flops 3628006656 | bytes 14174208 | tf_op jit(solution)/shard_map/dot_general | solution.py:214
  266.7 13.0 %convert_reduce_fusion = (f32[3072]{0:T(1024)S(1)}, bf16[768,3072]{1,0:T(8,128)(2,1)}) fusion(f32[768,3072]{1,0:T(8,128)} %get-tuple-element.117, f32[768,3072]{1,0:T(8,128)} %get-tuple-element.142, f32[3072]{0:T(1024)S(1)} %add.142, bf16[768,768]{0,1:T(8,128)(2,1)S(1)} %get-tuple-element.109, bf16[3072,768]{1,0:T(8,128)(2,1)S(1)} %bitcast.98), kind=kOutput, calls=%fused_computation.2 | convolution fusion | flops 3663983616 | bytes 29515776 | tf_op jit(solution)/shard_map/dot_general | solution.py:154
  279.7 7.3 %multiply_reduce_fusion = (f32[768]{0:T(1024)S(1)}, f32[768]{0:T(1024)S(1)}, f32[768]{0:T(1024)S(1)}, f32[768,768]{0,1:T(8,128)S(1)}) fusion(f32[768,768]{0,1:T(8,128)S(1)} %copy-done.3, f32[768]{0:T(1024)S(1)} %fusion.20, f32[768]{0:T(1024)S(1)} %broadcast_multiply_fusion.1, f32[768]{0:T(1024)S(1)} %mul.161, f32[768]{0:T(1024)S(1)} %negate_multiply_fusion.2, ...), kind=kOutput, calls=%fused_computation.38 | convolution fusion | flops 3633903360 | bytes 17728512 | tf_op jit(solution)/shard_map/dot_general | solution.py:154
  292.4 9.1 %convolution_convert_fusion.1 = bf16[768,3072]{1,0:T(8,128)(2,1)} fusion(bf16[768,3072]{1,0:T(8,128)(2,1)} %get-tuple-element.111, f32[768,768]{0,1:T(8,128)} %copy-done.2, f32[768]{0:T(1024)S(1)} %add.139, f32[768]{0:T(1024)S(1)} %mul.161, f32[768]{0:T(1024)S(1)} %fusion.20, f32[768]{0:T(1024)S(1)} %broadcast_multiply_fusion.1), kind=kOutput, calls=%fused_computation.19 | convolution fusion | flops 3629187072 | bytes 11808768 | tf_op jit(solution)/shard_map/dot_general | solution.py:154
  301.6 8.8 %convolution_convert_fusion = bf16[3072,768]{1,0:T(8,128)(2,1)} fusion(bf16[768,3072]{1,0:T(8,128)(2,1)} %get-tuple-element.116, bf16[768,768]{0,1:T(8,128)(2,1)} %copy-done.6), kind=kOutput, calls=%fused_computation.18 | convolution fusion | flops 3626237952 | bytes 10616832 | tf_op jit(solution)/shard_map/dot_general | solution.py:154
  326.2 8.2 %all-to-all-done.1 = bf16[4,192,768]{2,1,0:T(8,128)(2,1)} async-done(((bf16[4,192,768]{2,1,0:T(8,128)(2,1)}), bf16[4,192,768]{2,1,0:T(8,128)(2,1)}, u32[]{:S(2)}, u32[]{:S(2)}) %all-to-all-start.1) | async-done | bytes 1179680 | tf_op jit(solution)/shard_map/all_to_all | solution.py:230
  347.1 40.5 %attn_bwd.1 = (bf16[192,3072]{1,0:T(8,128)(2,1)}, bf16[3,3072,64]{2,1,0:T(8,128)(2,1)}, bf16[3,3072,64]{2,1,0:T(8,128)(2,1)}) custom-call(s32[1,8]{1,0:T(1,128)} %starts.3, bf16[192,3072]{1,0:T(8,128)(2,1)} %fusion.8.qT, bf16[3,3072,64]{2,1,0:T(8,128)(2,1)} %bitcast.79, bf16[3,3072,64]{2,1,0:T(8,128)(2,1)} %bitcast.76, bf16[192,3072]{1,0:T(8,128)(2,1)} %copy-done.5, ...), custom_call_target="tpu_custom_call" | custom-call | tf_op jit(solution)/shard_map/attn_bwd/pallas_call | solution.py:129
  395.3 7.3 %fusion.16 = bf16[768,576]{0,1:T(8,128)(2,1)} fusion(bf16[3072,768]{1,0:T(8,128)(2,1)} %all-gather.8.cloned.1.call-done, bf16[192,3072]{1,0:T(8,128)(2,1)} %bitcast.89, bf16[192,3072]{1,0:T(8,128)(2,1)} %bitcast.87, bf16[192,3072]{1,0:T(8,128)(2,1)} %get-tuple-element.26), kind=kOutput, calls=%fused_computation.58 | convolution fusion | flops 2728968192 | bytes 9142272 | tf_op jit(solution)/shard_map/dot_general | solution.py:154
  405.0 48.9 %reduce-scatter.12.cloned.1.call-done = bf16[96,3072]{1,0:T(8,128)(2,1)} async-done(((bf16[768,3072]{1,0:T(8,128)(2,1)}), bf16[96,3072]{1,0:T(8,128)(2,1)}) %reduce-scatter.12.cloned.1.call-update) | async-done | bytes 589840 | tf_op jit(solution)/shard_map/reduce_scatter | solution.py:258
  453.9 99.0 %reduce-scatter.14.cloned.1.call-done = bf16[384,768]{1,0:T(8,128)(2,1)} async-done(((bf16[3072,768]{1,0:T(8,128)(2,1)}), bf16[384,768]{1,0:T(8,128)(2,1)}) %reduce-scatter.14.cloned.1.call-update) | async-done | bytes 589840 | tf_op jit(solution)/shard_map/reduce_scatter | solution.py:258
  553.0 7.4 %convolution_convert_fusion.2 = bf16[3072,768]{0,1:T(8,128)(2,1)} fusion(bf16[768,576]{1,0:T(8,128)(2,1)S(1)} %copy-done.10, bf16[192,3072]{1,0:T(8,128)(2,1)} %bitcast.90, bf16[192,3072]{1,0:T(8,128)(2,1)} %bitcast.88, bf16[192,3072]{1,0:T(8,128)(2,1)} %get-tuple-element.26), kind=kOutput, calls=%fused_computation.20 | convolution fusion | flops 2730885120 | bytes 9142272 | tf_op jit(solution)/shard_map/dot_general | solution.py:154
  567.7 40.6 %psum.31 = f32[8,1152]{1,0:T(8,128)S(1)} all-reduce(f32[8,1152]{1,0:T(8,128)S(1)} %concatenate.15), channel_id=1, replica_groups=mesh['wshard'=8,'seq'=4] {'wshard','seq'}, use_global_device_ids=true, to_apply=%region_25.0 | all-reduce | flops 9216 | bytes 73728 | tf_op jit(solution)/shard_map/psum | solution.py:248
  609.5 11.1 %reduce-scatter.16.cloned.1.call-done = bf16[96,576]{1,0:T(8,128)(2,1)} async-done(((bf16[768,576]{1,0:T(8,128)(2,1)}), bf16[96,576]{1,0:T(8,128)(2,1)}) %reduce-scatter.16.cloned.1.call-update) | async-done | bytes 110608 | tf_op jit(solution)/shard_map/reduce_scatter | solution.py:261
  620.6 7.4 %all-gather.1 = bf16[384,576]{1,0:T(8,128)(2,1)S(1)} all-gather(bf16[96,576]{1,0:T(8,128)(2,1)} %reduce-scatter.16.cloned.1.call-done), channel_id=3, replica_groups=mesh['wshard'=8,'seq'=4] {'seq'}, dimensions={0}, use_global_device_ids=true | all-gather | bytes 552960 | tf_op jit(solution)/shard_map/all_gather | solution.py:262
  635.4 26.3 %all-reduce.3.cloned.1.call-done = (bf16[96,768]{1,0:T(8,128)(2,1)}, bf16[96,3072]{1,0:T(8,128)(2,1)}, bf16[384,768]{1,0:T(8,128)(2,1)}) async-done(((bf16[96,768]{1,0:T(8,128)(2,1)}, bf16[96,3072]{1,0:T(8,128)(2,1)}, bf16[384,768]{1,0:T(8,128)(2,1)}), (bf16[96,768]{1,0:T(8,128)(2,1)}, bf16[96,3072]{1,0:T(8,128)(2,1)}, bf16[384,768]{1,0:T(8,128)(2,1)})) %all-reduce.3.cloned.1.call-update) | async-done | bytes 1327120 | tf_op jit(solution)/shard_map/psum | solution.py:259
  666.9 45.1 %reduce-scatter.8.cloned.1.call-done = bf16[768,768]{0,1:T(8,128)(2,1)} async-done(((bf16[3072,768]{0,1:T(8,128)(2,1)}), bf16[768,768]{0,1:T(8,128)(2,1)}) %reduce-scatter.8.cloned.1.call-update) | async-done | bytes 1179664 | tf_op jit(solution)/shard_map/reduce_scatter | solution.py:236
  (162 shorter events, 102.1 us)
Async XLA Ops:
  7.2 38.8 %copy-start.13 = (bf16[96]{0:T(256)(128)(2,1)S(1)}, bf16[96]{0:T(256)(128)(2,1)}, u32[]{:S(2)}) copy-start(bf16[96]{0:T(256)(128)(2,1)} %param.27) | copy-start | bytes 580
  7.2 38.7 %copy-start.14 = (bf16[96]{0:T(256)(128)(2,1)S(1)}, bf16[96]{0:T(256)(128)(2,1)}, u32[]{:S(2)}) copy-start(bf16[96]{0:T(256)(128)(2,1)} %param.28) | copy-start | bytes 580
  7.2 38.7 %copy-start.15 = (bf16[96]{0:T(256)(128)(2,1)S(1)}, bf16[96]{0:T(256)(128)(2,1)}, u32[]{:S(2)}) copy-start(bf16[96]{0:T(256)(128)(2,1)} %param.29) | copy-start | bytes 580
  7.2 38.7 %copy-start.12 = (bf16[384]{0:T(512)(128)(2,1)S(1)}, bf16[384]{0:T(512)(128)(2,1)}, u32[]{:S(2)}) copy-start(bf16[384]{0:T(512)(128)(2,1)} %param.30) | copy-start | bytes 2308
  7.2 38.7 %copy-start.16 = (bf16[96]{0:T(256)(128)(2,1)S(1)}, bf16[96]{0:T(256)(128)(2,1)}, u32[]{:S(2)}) copy-start(bf16[96]{0:T(256)(128)(2,1)} %param.31) | copy-start | bytes 580
  7.3 38.7 %copy-start.17 = (bf16[96]{0:T(256)(128)(2,1)S(1)}, bf16[96]{0:T(256)(128)(2,1)}, u32[]{:S(2)}) copy-start(bf16[96]{0:T(256)(128)(2,1)} %param.32) | copy-start | bytes 580
  7.3 38.7 %copy-start.18 = (bf16[96]{0:T(256)(128)(2,1)S(1)}, bf16[96]{0:T(256)(128)(2,1)}, u32[]{:S(2)}) copy-start(bf16[96]{0:T(256)(128)(2,1)} %param.33) | copy-start | bytes 580
  7.3 38.7 %copy-start.19 = (bf16[96]{0:T(256)(128)(2,1)S(1)}, bf16[96]{0:T(256)(128)(2,1)}, u32[]{:S(2)}) copy-start(bf16[96]{0:T(256)(128)(2,1)} %param.34) | copy-start | bytes 580
  7.3 38.7 %copy-start.20 = (bf16[96]{0:T(256)(128)(2,1)S(1)}, bf16[96]{0:T(256)(128)(2,1)}, u32[]{:S(2)}) copy-start(bf16[96]{0:T(256)(128)(2,1)} %param.35) | copy-start | bytes 580
  7.3 70.1 %all-gather.8.cloned.1.call-start = ((), (), s32[]{:S(2)}) async-start(), calls=%async_computation.7 | async-start | bytes 5898240 | tf_op jit(solution)/shard_map/all_gather | solution.py:190
  8.0 132.1 %all-gather.10.cloned.1.call-start = ((), (), s32[]{:S(2)}) async-start(), calls=%async_computation.8 | async-start | bytes 1327104 | tf_op jit(solution)/shard_map/all_gather | solution.py:179
  8.8 164.7 %all-gather.12.cloned.1.call-start = ((), (), s32[]{:S(2)}) async-start(), calls=%async_computation.9 | async-start | bytes 5308416 | tf_op jit(solution)/shard_map/all_gather | solution.py:179
  9.5 243.8 %all-gather.14.cloned.1.call-start = ((), (), s32[]{:S(2)}) async-start(), calls=%async_computation.10 | async-start | bytes 5308416 | tf_op jit(solution)/shard_map/all_gather | solution.py:179
  46.0 39.5 %copy-start.9 = (bf16[768,576]{1,0:T(8,128)(2,1)}, bf16[768,576]{1,0:T(8,128)(2,1)S(1)}, u32[]{:S(2)}) copy-start(bf16[768,576]{1,0:T(8,128)(2,1)S(1)} %all_gather.27) | copy-start | bytes 2654212
  87.5 42.5 %copy-start.5 = (bf16[192,3072]{1,0:T(8,128)(2,1)}, bf16[192,3072]{1,0:T(8,128)(2,1)S(1)}, u32[]{:S(2)}) copy-start(bf16[192,3072]{1,0:T(8,128)(2,1)S(1)} %convolution_convert_fusion.3.kT) | copy-start | bytes 3538948
  132.5 20.3 %all-to-all-start = ((bf16[192,4,768]{2,0,1:T(8,128)(2,1)}), bf16[192,4,768]{2,0,1:T(8,128)(2,1)}, u32[]{:S(2)}, u32[]{:S(2)}) async-start(bf16[192,4,768]{2,0,1:T(8,128)(2,1)} %bitcast.73), calls=%async_computation | async-start | bytes 2359296 | tf_op jit(solution)/shard_map/all_to_all | solution.py:206
  137.0 268.1 %reduce-scatter.10.cloned.1.call-start = ((), (), s32[]{:S(2)}) async-start(), calls=%async_computation.12 | async-start | bytes 1327104 | tf_op jit(solution)/shard_map/reduce_scatter | solution.py:258
  292.4 161.5 %reduce-scatter.12.cloned.1.call-start = ((), (), s32[]{:S(2)}) async-start(), calls=%async_computation.13 | async-start | bytes 5308416 | tf_op jit(solution)/shard_map/reduce_scatter | solution.py:258
  301.6 251.3 %reduce-scatter.14.cloned.1.call-start = ((), (), s32[]{:S(2)}) async-start(), calls=%async_computation.14 | async-start | bytes 5308416 | tf_op jit(solution)/shard_map/reduce_scatter | solution.py:258
  314.3 20.2 %all-to-all-start.1 = ((bf16[4,192,768]{2,1,0:T(8,128)(2,1)}), bf16[4,192,768]{2,1,0:T(8,128)(2,1)}, u32[]{:S(2)}, u32[]{:S(2)}) async-start(bf16[4,192,768]{2,1,0:T(8,128)(2,1)} %bitcast.91), calls=%async_computation.1 | async-start | bytes 2359296 | tf_op jit(solution)/shard_map/all_to_all | solution.py:230
  318.5 302.1 %reduce-scatter.16.cloned.1.call-start = ((), (), s32[]{:S(2)}) async-start(), calls=%async_computation.15 | async-start | bytes 1105920 | tf_op jit(solution)/shard_map/reduce_scatter | solution.py:261
  402.6 150.3 %copy-start.10 = (bf16[768,576]{1,0:T(8,128)(2,1)S(1)}, bf16[768,576]{1,0:T(8,128)(2,1)}, u32[]{:S(2)}) copy-start(bf16[768,576]{1,0:T(8,128)(2,1)} %copy-done.9) | copy-start | bytes 2654212
  405.0 256.8 %all-reduce.3.cloned.1.call-start = ((), (), s32[]{:S(2)}) async-start(), calls=%async_computation.16 | async-start | bytes 2654208 | tf_op jit(solution)/shard_map/psum | solution.py:259
  552.9 159.1 %reduce-scatter.8.cloned.1.call-start = ((), (), s32[]{:S(2)}) async-start(), calls=%async_computation.11 | async-start | bytes 5898240 | tf_op jit(solution)/shard_map/reduce_scatter | solution.py:236
  (14 other events, 97.7 us)
Sparse Core Ops, SparseCore 0:
  9.7 40.1 all-gather.7
  52.0 41.3 all-gather.9
  95.6 77.8 all-gather.11
  175.5 77.6 all-gather.13
  292.5 63.1 reduce-scatter.9
  359.2 94.6 reduce-scatter.11
  457.6 95.2 reduce-scatter.13
  556.8 63.7 reduce-scatter.15
  623.2 38.4 all-reduce.2
  664.1 47.7 reduce-scatter.7

commit v2 on v1

--- a/solution.py
+++ b/solution.py
@@ -8,10 +8,10 @@
 from jax.sharding import PartitionSpec as P
 
 NORM_EPS = 1e-05
-
 HD = 64
 bf = jnp.bfloat16
 f32 = jnp.float32
+
 
 def doc_bounds(starts_ref, pos, total):
     lo = jnp.zeros_like(pos); hi = jnp.full_like(pos, total)
@@ -139,6 +139,305 @@
     )(starts, qT, q3, k3, kT, v3, doT, do3, oT, lse)
 
 
+MESH = pl.DeviceIdType.MESH
+
+
+class Wire:
+    def __init__(self, send, recv):
+        self.send, self.recv, self.used, self.open = send, recv, 0, []
+
+    def slot(self):
+        self.used += 1
+        return self.used - 1
+
+    def start(self, slot, src, dst, device):
+        copy = pltpu.make_async_remote_copy(
+            src_ref=src, dst_ref=dst, send_sem=self.send.at[slot], recv_sem=self.recv.at[slot],
+            device_id=device, device_id_type=MESH,
+        )
+        copy.start()
+        self.open.append(copy)
+
+    def arrived(self, slot, dst, device):
+        pltpu.make_async_remote_copy(
+            src_ref=dst, dst_ref=dst, send_sem=self.send.at[slot], recv_sem=self.recv.at[slot],
+            device_id=device, device_id_type=MESH,
+        ).wait_recv()
+
+    def drain(self):
+        for copy in self.open:
+            copy.wait_send()
+        self.open = []
+
+
+def grid_peers():
+    shard, seq = lax.axis_index("wshard"), lax.axis_index("seq")
+    z, y = shard // 2, shard % 2
+    x, c = seq // 2, seq % 2
+    at = lambda zz, yy, xx, cc: (zz * 2 + yy, xx * 2 + cc)
+    along = [at((z + d) % 4, y, x, c) for d in range(4)]
+    return z, y, x, c, along, at(z, 1 - y, x, c), at(z, y, 1 - x, c), at(z, y, x, 1 - c)
+
+
+def greet(peers):
+    barrier = pltpu.get_barrier_semaphore()
+    for peer in peers:
+        pl.semaphore_signal(barrier, inc=1, device_id=peer, device_id_type=MESH)
+    pl.semaphore_wait(barrier, len(peers))
+
+
+ORDER = (1, 3, 2)
+SHARE = 80
+
+
+def gather_kernel(a_ref, b_ref, t_ref, g_ref, q_ref, x_ref, send, recv, lsem):
+    z, y, x, c, along, ypeer, xpeer, cpeer = grid_peers()
+    own = z * 2 + y
+    rows = a_ref.shape[0]
+    half = rows // 2
+    plain = half - 2 * SHARE
+    wire = Wire(send, recv)
+    spot = lambda r, d: ((z + 4 - d) % 4) * 2 + (y if r == 0 else 1 - y)
+    base, other = half * c, half * (1 - c)
+    nspan = pl.ds(pl.multiple_of(base, 16), plain)
+    dspan = pl.ds(pl.multiple_of(base + plain + SHARE * x, 16), SHARE)
+    xspan = pl.ds(pl.multiple_of(base + plain + SHARE * (1 - x), 16), SHARE)
+    pn = pl.ds(pl.multiple_of(other, 16), plain)
+    pd = pl.ds(pl.multiple_of(other + plain + SHARE * x, 16), SHARE)
+    px = pl.ds(pl.multiple_of(other + plain + SHARE * (1 - x), 16), SHARE)
+    seq = x * 2 + c
+    locals_ = [
+        pltpu.make_async_copy(a_ref, g_ref.at[own], lsem.at[0]),
+        pltpu.make_async_copy(b_ref, q_ref.at[own], lsem.at[1]),
+        pltpu.make_async_copy(t_ref, x_ref.at[seq], lsem.at[2]),
+    ]
+    for copy in locals_:
+        copy.start()
+    greet(along[1:] + [ypeer, xpeer, cpeer])
+    S = {}
+    for name in ("zB", "zN", "zD", "yB", "yN", "yD"):
+        S[name] = [wire.slot() for _ in range(4)]
+    for name in ("cN", "cD", "cX", "xD"):
+        S[name] = [[wire.slot() for _ in range(4)] for _ in range(2)]
+    tx, tc0, tc1 = wire.slot(), wire.slot(), wire.slot()
+    wire.start(tx, t_ref, x_ref.at[seq], xpeer)
+    for d in ORDER:
+        wire.start(S["zB"][d], b_ref, q_ref.at[own], along[d])
+    wire.start(S["yB"][0], b_ref, q_ref.at[own], ypeer)
+    for d in ORDER:
+        wire.start(S["zN"][d], a_ref.at[nspan], g_ref.at[own, nspan], along[d])
+    wire.start(S["yN"][0], a_ref.at[nspan], g_ref.at[own, nspan], ypeer)
+    for d in ORDER:
+        wire.start(S["zD"][d], a_ref.at[dspan], g_ref.at[own, dspan], along[d])
+    wire.start(S["yD"][0], a_ref.at[dspan], g_ref.at[own, dspan], ypeer)
+    wire.start(tc0, t_ref, x_ref.at[seq], cpeer)
+    for d in ORDER:
+        w = spot(0, d)
+        wire.arrived(S["zB"][d], q_ref.at[w], along[d])
+        wire.start(S["yB"][d], q_ref.at[w], q_ref.at[w], ypeer)
+    for d in ORDER:
+        w = spot(0, d)
+        wire.arrived(S["zN"][d], g_ref.at[w, nspan], along[d])
+        wire.start(S["yN"][d], g_ref.at[w, nspan], g_ref.at[w, nspan], ypeer)
+        wire.start(S["cN"][0][d], g_ref.at[w, nspan], g_ref.at[w, nspan], cpeer)
+    xtok = (1 - x) * 2 + c
+    wire.arrived(tx, x_ref.at[xtok], xpeer)
+    wire.start(tc1, x_ref.at[xtok], x_ref.at[xtok], cpeer)
+    for d in ORDER:
+        w = spot(0, d)
+        wire.arrived(S["zD"][d], g_ref.at[w, dspan], along[d])
+        for slot, peer in ((S["yD"][d], ypeer), (S["xD"][0][d], xpeer), (S["cD"][0][d], cpeer)):
+            wire.start(slot, g_ref.at[w, dspan], g_ref.at[w, dspan], peer)
+    for d in (0,) + ORDER:
+        w = spot(1, d)
+        wire.arrived(S["yN"][d], g_ref.at[w, nspan], ypeer)
+        wire.start(S["cN"][1][d], g_ref.at[w, nspan], g_ref.at[w, nspan], cpeer)
+        wire.arrived(S["yB"][d], q_ref.at[w], ypeer)
+    for d in (0,) + ORDER:
+        w = spot(1, d)
+        wire.arrived(S["yD"][d], g_ref.at[w, dspan], ypeer)
+        for slot, peer in ((S["xD"][1][d], xpeer), (S["cD"][1][d], cpeer)):
+            wire.start(slot, g_ref.at[w, dspan], g_ref.at[w, dspan], peer)
+    rest = [(0, d) for d in ORDER] + [(1, d) for d in (0,) + ORDER]
+    for r, d in rest:
+        w = spot(r, d)
+        wire.arrived(S["xD"][r][d], g_ref.at[w, xspan], xpeer)
+        wire.start(S["cX"][r][d], g_ref.at[w, xspan], g_ref.at[w, xspan], cpeer)
+    wire.arrived(tc0, x_ref.at[x * 2 + 1 - c], cpeer)
+    wire.arrived(tc1, x_ref.at[(1 - x) * 2 + 1 - c], cpeer)
+    for r, d in rest:
+        w = spot(r, d)
+        wire.arrived(S["cN"][r][d], g_ref.at[w, pn], cpeer)
+        wire.arrived(S["cD"][r][d], g_ref.at[w, pd], cpeer)
+        wire.arrived(S["cX"][r][d], g_ref.at[w, px], cpeer)
+    wire.drain()
+    for copy in locals_:
+        copy.wait()
+
+
+def gather_inputs(a, b, tokens):
+    slots = 59 + 3 + 12
+    hbm = pl.BlockSpec(memory_space=pl.ANY)
+    vmem = pl.BlockSpec(memory_space=pltpu.VMEM)
+    return pl.pallas_call(
+        gather_kernel,
+        in_specs=[vmem] * 3, out_specs=[hbm] * 3,
+        out_shape=[jax.ShapeDtypeStruct((8,) + a.shape, a.dtype), jax.ShapeDtypeStruct((8,) + b.shape, b.dtype),
+                   jax.ShapeDtypeStruct((4,) + tokens.shape, tokens.dtype)],
+        scratch_shapes=[pltpu.SemaphoreType.DMA((slots,)), pltpu.SemaphoreType.DMA((slots,)), pltpu.SemaphoreType.DMA((3,))],
+        compiler_params=pltpu.CompilerParams(collective_id=1, has_side_effects=True),
+        name="gather_inputs",
+    )(a, b, tokens)
+
+
+def add_rows(dst, parts, rows, step=16):
+    def body(i, _):
+        at = pl.ds(pl.multiple_of(i * step, step), step)
+        total = parts[0][at, :].astype(f32)
+        for part in parts[1:]:
+            total = total + part[at, :].astype(f32)
+        dst[at, :] = total.astype(dst.dtype)
+        return 0
+    lax.fori_loop(0, rows // step, body, 0)
+
+
+ALL = ORDER + (0,)
+
+
+def reduce_kernel(ga, gb, dx, sm, fa, fb, fx, fr, fs, rc, rd, ry, ryd, rz, rzd, hb, ryb, rzb, hx, rxc,
+                  hs, rys, rzs, s1, s2, s3, s4, fn, rn, send, recv):
+    z, y, x, c, along, ypeer, xpeer, cpeer = grid_peers()
+    half = ga.shape[2] // 2
+    plain = half - 2 * SHARE
+    base, other = pl.multiple_of(half * c, 16), pl.multiple_of(half * (1 - c), 16)
+    mine, theirs = pl.multiple_of(plain + SHARE * x, 16), pl.multiple_of(plain + SHARE * (1 - x), 16)
+    nrow = pl.ds(0, plain)
+    wire = Wire(send, recv)
+    new4 = lambda: [wire.slot() for _ in range(4)]
+    kc = [new4(), new4()]
+    kcx, kx, kxd = new4(), wire.slot(), new4()
+    kyn, kyd, kyb, kys = new4(), new4(), wire.slot(), wire.slot()
+    kzn, kzd, kzb, kzs = new4(), new4(), new4(), new4()
+    fin = [wire.slot() for _ in range(13)]
+    zz = lambda d: (z + d) % 4
+    greet(along[1:] + [ypeer, xpeer, cpeer])
+    wire.start(kys, sm.at[:, 1 - y], rys, ypeer)
+    wire.start(kyb, gb.at[:, 1 - y], ryb, ypeer)
+    for i, d in enumerate(ALL):
+        for r in (1, 0):
+            yy = y if r == 0 else 1 - y
+            wire.start(kc[r][d], ga.at[zz(d), yy, pl.ds(other, half)], rc.at[zz(d), yy], cpeer)
+        if i == 0:
+            for t in range(2):
+                wire.start(kcx[t], dx.at[t, 1 - c], rxc.at[t], cpeer)
+    for d in ALL:
+        for r in (1, 0):
+            yy = y if r == 0 else 1 - y
+            blk = rc.at[zz(d), yy]
+            wire.arrived(kc[r][d], blk, cpeer)
+            add_rows(blk, [ga.at[zz(d), yy, pl.ds(base, half)], blk], half)
+        wire.start(kxd[d], rc.at[zz(d), :, pl.ds(theirs, SHARE)], rd.at[zz(d)], xpeer)
+        wire.start(kyn[d], rc.at[zz(d), 1 - y, nrow], ry.at[zz(d)], ypeer)
+    for t in range(2):
+        wire.arrived(kcx[t], rxc.at[t], cpeer)
+        add_rows(hx.at[t], [dx.at[t, c], rxc.at[t]], hx.shape[1])
+    wire.start(kx, hx.at[1 - x], fr, xpeer)
+    wire.arrived(kys, rys, ypeer)
+    wire.arrived(kyb, ryb, ypeer)
+    for d in ALL:
+        hs[d] = sm[zz(d), y] + rys[zz(d)]
+        add_rows(hb.at[d], [gb.at[zz(d), y], ryb.at[zz(d)]], hb.shape[1])
+        if d:
+            wire.start(kzs[d], hs.at[d], rzs.at[d], along[d])
+            wire.start(kzb[d], hb.at[d], rzb.at[d], along[d])
+    for d in ALL:
+        wire.arrived(kxd[d], rd.at[zz(d)], xpeer)
+        for yy in range(2):
+            spot = rc.at[zz(d), yy, pl.ds(mine, SHARE)]
+            add_rows(spot, [spot, rd.at[zz(d), yy]], SHARE)
+        wire.start(kyd[d], rc.at[zz(d), 1 - y, pl.ds(mine, SHARE)], ryd.at[zz(d)], ypeer)
+    for d in ALL:
+        wire.arrived(kyn[d], ry.at[zz(d)], ypeer)
+        spot = rc.at[zz(d), y, nrow]
+        add_rows(spot, [spot, ry.at[zz(d)]], plain)
+        if d:
+            wire.start(kzn[d], spot, rz.at[d], along[d])
+    for d in ALL:
+        wire.arrived(kyd[d], ryd.at[zz(d)], ypeer)
+        spot = rc.at[zz(d), y, pl.ds(mine, SHARE)]
+        add_rows(spot, [spot, ryd.at[zz(d)]], SHARE)
+        if d:
+            wire.start(kzd[d], spot, rzd.at[d], along[d])
+    for d in ORDER:
+        wire.arrived(kzs[d], rzs.at[d], along[d])
+        wire.arrived(kzb[d], rzb.at[d], along[d])
+    s1[...] = hs[0] + rzs[1] + rzs[2] + rzs[3]
+    wire.start(fin[0], s1, s2, xpeer)
+    seq, xseq = 2 * x + c, 2 * (1 - x) + c
+    add_rows(fb.at[seq], [hb.at[0]] + [rzb.at[d] for d in ORDER], hb.shape[1])
+    wire.start(fin[1], fb.at[seq], fb.at[seq], xpeer)
+    wire.start(fin[2], fb.at[seq], fb.at[seq], cpeer)
+    wire.arrived(fin[0], s2, xpeer)
+    s3[...] = s1[...] + s2[...]
+    wire.start(fin[3], s3, s4, cpeer)
+    wire.arrived(fin[1], fb.at[xseq], xpeer)
+    wire.start(fin[4], fb.at[xseq], fb.at[xseq], cpeer)
+    for d in ORDER:
+        wire.arrived(kzn[d], rz.at[d], along[d])
+    add_rows(fn, [rc.at[z, y, nrow]] + [rz.at[d] for d in ORDER], plain)
+    wire.start(fin[5], fn, rn, xpeer)
+    for d in ORDER:
+        wire.arrived(kzd[d], rzd.at[d], along[d])
+    dmine = pl.ds(pl.multiple_of(base + mine, 16), SHARE)
+    dtheirs = pl.ds(pl.multiple_of(base + theirs, 16), SHARE)
+    add_rows(fa.at[dmine], [rc.at[z, y, pl.ds(mine, SHARE)]] + [rzd.at[d] for d in ORDER], SHARE)
+    wire.start(fin[6], fa.at[dmine], fa.at[dmine], xpeer)
+    wire.start(fin[7], fa.at[dmine], fa.at[dmine], cpeer)
+    wire.arrived(fin[5], rn, xpeer)
+    nspan = pl.ds(base, plain)
+    add_rows(fa.at[nspan], [fn, rn], plain)
+    wire.start(fin[8], fa.at[nspan], fa.at[nspan], cpeer)
+    wire.arrived(fin[6], fa.at[dtheirs], xpeer)
+    wire.start(fin[9], fa.at[dtheirs], fa.at[dtheirs], cpeer)
+    wire.arrived(kx, fr, xpeer)
+    fx[...] = hx[x]
+    wire.arrived(fin[3], s4, cpeer)
+    fs[...] = s3[...] + s4[...]
+    wire.arrived(fin[2], fb.at[2 * x + 1 - c], cpeer)
+    wire.arrived(fin[4], fb.at[2 * (1 - x) + 1 - c], cpeer)
+    wire.arrived(fin[8], fa.at[pl.ds(other, plain)], cpeer)
+    wire.arrived(fin[7], fa.at[pl.ds(pl.multiple_of(other + mine, 16), SHARE)], cpeer)
+    wire.arrived(fin[9], fa.at[pl.ds(pl.multiple_of(other + theirs, 16), SHARE)], cpeer)
+    wire.drain()
+
+
+def reduce_grads(ga, gb, dx, sm):
+    rows, cols = ga.shape[1:]
+    half = rows // 2
+    plain = half - 2 * SHARE
+    toks = dx.shape[1]
+    vmem = pl.BlockSpec(memory_space=pltpu.VMEM)
+    b0, b1 = gb.shape[1:]
+    V = pltpu.VMEM
+    sv = lambda *lead: V(lead + sm.shape[1:], f32)
+    slots = 64
+    return pl.pallas_call(
+        reduce_kernel,
+        in_specs=[vmem] * 4, out_specs=[vmem] * 5,
+        out_shape=[jax.ShapeDtypeStruct((rows, cols), bf), jax.ShapeDtypeStruct((4, b0, b1), bf),
+                   jax.ShapeDtypeStruct((toks, cols), bf), jax.ShapeDtypeStruct((toks, cols), bf),
+                   jax.ShapeDtypeStruct(sm.shape[1:], f32)],
+        scratch_shapes=[V((4, 2, half, cols), bf), V((4, 2, SHARE, cols), bf), V((4, plain, cols), bf), V((4, SHARE, cols), bf),
+                        V((4, plain, cols), bf), V((4, SHARE, cols), bf),
+                        V((4, b0, b1), bf), V((4, b0, b1), bf), V((4, b0, b1), bf),
+                        V((2, toks, cols), bf), V((2, toks, cols), bf),
+                        sv(4), sv(4), sv(4), sv(), sv(), sv(), sv(), V((plain, cols), bf), V((plain, cols), bf),
+                        pltpu.SemaphoreType.DMA((slots,)), pltpu.SemaphoreType.DMA((slots,))],
+        compiler_params=pltpu.CompilerParams(collective_id=2, has_side_effects=True, vmem_limit_bytes=67043328),
+        name="reduce_grads",
+    )(ga.reshape((4, 2) + ga.shape[1:]), gb.reshape((4, 2) + gb.shape[1:]), dx.reshape((2, 2) + dx.shape[1:]), sm.reshape((4, 2) + sm.shape[1:]))
+
+
 def layer_norm(inputs, norm_gain, norm_bias):
     row_mean = jnp.mean(inputs, axis=-1, keepdims=True)
     centred = inputs - row_mean
@@ -156,6 +455,30 @@
         right_in,
         (((left_dim,), (right_dim,)), ((), ())),
         preferred_element_type=jnp.float32,
+    )
+
+
+def chips_of_two_by_four():
+    return lax.axis_size("wshard") == 8 and lax.axis_size("seq") == 4
+
+
+def gather_parts(a, b, tokens):
+    if chips_of_two_by_four():
+        return gather_inputs(a, b, tokens)
+    return lax.all_gather(a, "wshard"), lax.all_gather(b, "wshard"), lax.all_gather(tokens, "seq")
+
+
+def reduce_parts(ga, gb, dx, sm):
+    if chips_of_two_by_four():
+        return reduce_grads(ga, gb, dx, sm)
+
+    def scatter(part):
+        return lax.psum_scatter(part, "wshard", scatter_dimension=0, tiled=False)
+
+    fx = lax.psum_scatter(dx, "seq", scatter_dimension=0, tiled=False)
+    return (
+        lax.psum(scatter(ga), "seq"), lax.all_gather(scatter(gb), "seq"), fx, jnp.zeros_like(fx),
+        lax.psum(scatter(sm), "seq"),
     )
 
 
@@ -166,30 +489,37 @@
     gain_first, bias_first, gain_second, bias_second,
 ):
     model = tokens.shape[1]
+    rows = w_query.shape[0]
+    shards_n = lax.axis_size("wshard")
     seq_n = lax.axis_size("seq")
     seq_i = lax.axis_index("seq")
-    shard_i = lax.axis_index("wshard")
     width = model // seq_n
     heads = width // HD
+    wide = w_inner.shape[1] // model
 
     def own(columns):
         return lax.dynamic_slice_in_dim(columns, seq_i * width, width, columns.ndim - 1)
 
-    def gather(shard):
-        return lax.all_gather(shard, "wshard", axis=0, tiled=True)
-
-    smalls = (b_query, b_value, b_output, b_inner, b_outer, gain_first, bias_first, gain_second, bias_second)
-    sizes = [member.shape[0] for member in smalls]
-    packed = lax.all_gather(jnp.concatenate(smalls), "wshard", axis=0, tiled=False).astype(f32)
-    full, at = [], 0
-    for size in sizes:
-        full.append(packed[:, at:at + size].reshape(-1))
-        at += size
-    bias_query, bias_value, bias_output, bias_inner, bias_outer, gain_one, shift_one, gain_two, shift_two = full
-
-    stream = lax.all_gather(tokens, "seq", axis=0, tiled=True)
-    w_own = gather(jnp.concatenate([own(w_query), own(w_key), own(w_value)], axis=1))
-    output_full, inner_full, outer_full = gather(w_output), gather(w_inner), gather(w_outer)
+    smalls = (b_query, b_value, b_output, b_outer, gain_first, bias_first, gain_second, bias_second)
+    small_cols = jnp.stack(smalls + tuple(b_inner.reshape(wide, rows)), axis=1)
+    cols_n = small_cols.shape[1]
+    a = jnp.concatenate(
+        [w_output, w_inner.reshape(rows, wide, model).transpose(1, 0, 2).reshape(wide * rows, model), w_outer], axis=0
+    )
+    b = jnp.concatenate([own(w_query), own(w_key), own(w_value), jnp.pad(small_cols, ((0, 0), (0, HD - cols_n)))], axis=1)
+    big, side, stream = gather_parts(a, b, tokens)
+    stream = stream.reshape(-1, model)
+    side = side.reshape(model, -1)
+    w_own = side[:, :3 * width]
+    vectors = side[:, 3 * width:3 * width + cols_n].astype(f32).T
+    bias_query, bias_value, bias_output, bias_outer, gain_one, shift_one, gain_two, shift_two = vectors[:8]
+    bias_inner = vectors[8:].reshape(wide, shards_n, rows).transpose(1, 0, 2).reshape(-1)
+    output_full = big[:, :rows].reshape(model, model)
+    inner_full = jnp.concatenate(
+        [big[:, (1 + j) * rows:(2 + j) * rows].reshape(model, model) for j in range(wide)], axis=1
+    )
+    outer_full = big[:, (1 + wide) * rows:].reshape(-1, model)
+
     scale = HD ** -0.5
     qT = ((contract(w_own[:, :width], stream, 0, 1) + own(bias_query)[:, None]).astype(bf) * bf(scale))
     kT = contract(w_own[:, width:2 * width], stream, 0, 1).astype(bf)
@@ -231,41 +561,41 @@
 
     dqT, dk3, dv3 = attn_bwd(starts, qT, q3, k3, kT, v3, doT, by_token(doT), oT, lse, 256, 512)
     dT = jnp.concatenate([dqT, by_feature(dk3), by_feature(dv3)], axis=0)
-    grad_own = contract(stream, dT, 0, 1).astype(bf)
-    d_part = contract(dT, w_own, 0, 1).astype(bf)
-    d_tokens = lax.psum_scatter(d_part, "seq", scatter_dimension=0, tiled=True).astype(f32) + d_resid
+    gb = contract(stream, dT, 0, 1).astype(bf).reshape(shards_n, rows, -1)
+    dx = contract(dT, w_own, 0, 1).astype(bf).reshape(seq_n, -1, model)
+    by_rows = lambda grad: grad.astype(bf).reshape(shards_n, -1, model)
+    ga = jnp.concatenate(
+        [by_rows(grad_output)] + [by_rows(grad_inner[:, j * model:(j + 1) * model]) for j in range(wide)]
+        + [by_rows(grad_outer)], axis=1,
+    )
 
     def spread(own_sum):
         return lax.dynamic_update_slice(jnp.zeros((model,), f32), own_sum, (seq_i * width,))
 
-    grad_small = (
+    small_rows = (
         spread(jnp.sum(dqT.astype(f32), axis=1)),
         spread(jnp.sum(dv3.astype(f32), axis=1).reshape(-1)),
-        grad_bias_output, grad_bias_inner, grad_bias_outer,
-        grad_gain_one, grad_bias_one, grad_gain_two, grad_bias_two,
-    )
-    shards_n = lax.axis_size("wshard")
-    small_sum = lax.psum(
-        jnp.concatenate([member.reshape(shards_n, -1) for member in grad_small], axis=1), ("wshard", "seq")
-    )
-    small_own = lax.dynamic_index_in_dim(small_sum, shard_i, 0, keepdims=False)
-    outs, at = [], 0
-    for size in sizes:
-        outs.append(small_own[at:at + size])
-        at += size
-
-    def scatter(grad):
-        low = lax.psum_scatter(grad.astype(bf), "wshard", scatter_dimension=0, tiled=True)
-        return lax.psum(low, "seq").astype(f32)
-
-    own_shard = lax.psum_scatter(grad_own, "wshard", scatter_dimension=0, tiled=True)
-    parts = lax.all_gather(own_shard, "seq", axis=0, tiled=False).astype(f32)
-    qkv_grads = [
-        parts[:, :, i * width:(i + 1) * width].transpose(1, 0, 2).reshape(-1, model) for i in range(3)
+        grad_bias_output, grad_bias_outer, grad_gain_one, grad_bias_one, grad_gain_two, grad_bias_two,
+    )
+    sm = jnp.concatenate(
+        [jnp.stack([row.reshape(shards_n, rows) for row in small_rows], axis=1),
+         grad_bias_inner.reshape(shards_n, wide, rows)], axis=1,
+    )
+    sm = jnp.pad(sm, ((0, 0), (0, -cols_n % 8), (0, -rows % 128)))
+    fa, fb, fx, fr, fs = reduce_parts(ga, gb, dx, sm)
+    d_tokens = fx.astype(f32) + fr.astype(f32) + d_resid
+    fb = fb.astype(f32)
+    grads = [
+        jnp.concatenate([fb[s, :, i * width:(i + 1) * width] for s in range(seq_n)], axis=1) for i in range(3)
     ]
+    fa = fa.astype(f32)
+    g_inner = jnp.concatenate([fa[(1 + j) * rows:(2 + j) * rows] for j in range(wide)], axis=1)
+    tail = [fs[i, :rows] for i in range(8)]
+    g_b_inner = fs[8:8 + wide, :rows].reshape(-1)
     return (
-        layer_result.astype(bf), d_tokens, *qkv_grads,
-        scatter(grad_output), scatter(grad_inner), scatter(grad_outer), *outs,
+        layer_result.astype(bf), d_tokens, *grads,
+        fa[:rows], g_inner, fa[(1 + wide) * rows:],
+        tail[0], tail[1], tail[2], g_b_inner, *tail[3:],
     )
 
 

time: 732 us -> 481 us (0.66)
  waiting for transfers between devices: 320 us -> 0.82 us
  Pallas kernels: 80.6 us -> 279 us
  blocking collectives: 113 us -> 0 us
  between operations: 14.9 us -> 1.52 us
  matrix products: 112 us -> 101 us
    reduce_scatter x5 -> x0, waiting for transfers between devices: 204 us -> none  [the longest x3 148 us: scatter(): lax.psum_scatter(grad.astype(bf), 'wshard', scatter_dimension=0, tiled=True)]
    pallas_call x0 -> x2, Pallas kernels: none -> 187 us  [the longest x1 100 us: reduce_grads(): pl.pallas_call(reduce_kernel, in_specs=[vmem] * 4, out_specs=[vmem] * 5,...]
    all_gather x3 -> x0, blocking collectives: 72.9 us -> none  [the longest x1 34.6 us: gather(): return lax.all_gather(shard, 'wshard', axis=0, tiled=True)]
    all_gather x4 -> x0, waiting for transfers between devices: 65.8 us -> none  [the longest x3 65.8 us: gather(): return lax.all_gather(shard, 'wshard', axis=0, tiled=True)]
    psum x1 -> x0, blocking collectives: 40.6 us -> none  [shards(): lax.psum(jnp.concatenate([member.reshape(shards_n, -1) for member in grad...]
    psum x1 -> x0, waiting for transfers between devices: 26.3 us -> none  [scatter(): return lax.psum(low, 'seq').astype(f32)]
    slice x4 -> x8, local copies, waits for them, and re-layouts: 1.43 us -> 16.5 us  [the longest x1 4.85 us: shards(): outer_full = big[:, (1 + wide) * rows:].reshape(-1, model)]
    all_to_all x1, waiting for transfers between devices: 12.7 us -> 0.82 us  [shards(): mixed = lax.all_to_all(mixT, 'seq', split_axis=1, concat_axis=0, tiled=True)]
  transfers between devices with their start and end apart: 12 -> 2, of which waited for: 9 -> 1; matrix products, arithmetic and copies ran while one was open for 19% -> 7% of each run, Pallas kernels for 11% -> 0%
where the time goes in v2:
time: 481 us; the launch traced here: 473 us
  Pallas kernels  279 us (58%)
  matrix products  101 us (21%)
  local copies, waits for them, and re-layouts  62.8 us (13%)
  other arithmetic  20.2 us (4%)
  starting transfers between devices  7.81 us (2%)
    pallas_call x1, Pallas kernels, reduce_grads(): pl.pallas_call(reduce_kernel, in_specs=[vmem] * 4, out_specs=[vmem] * 5,...  100 us
    pallas_call x1, Pallas kernels, gather_inputs(): pl.pallas_call(gather_kernel, in_specs=[vmem] * 3, out_specs=[hbm] * 3, o...  86.3 us
    dot_general x12, matrix products, contract(): lax.dot_general(left_in, right_in, (((left_dim,), (right_dim,)), ((), ())...  63.5 us
    pallas_call x1, Pallas kernels, attn_fwd(): pl.pallas_call(functools.partial(fwd_kernel, heads, bq, bk), grid=(total...  48.1 us
    pallas_call x1, Pallas kernels, attn_bwd(): pl.pallas_call(functools.partial(bwd_kernel, heads, bq, bk), grid=(total...  44.7 us
    dot_general x1, matrix products, shards(): jnp.dot(first_low, inner_full, preferred_element_type=f32) + bias_inner  31.3 us
    reshape x5, local copies, waits for them, and re-layouts, by_token(): return arr.reshape(heads, HD, -1).transpose(0, 2, 1)  10.5 us
  transfers between devices with their start and end apart: 2, of which 1 were waited for; matrix products, arithmetic and copies ran while one was open for 7% of the time, Pallas kernels for 0%

profile of v2, /device:TPU:0, one launch (start us, length us, event | category | flops | bytes accessed | tf_op | source)
XLA Modules:
  0.0 473.5 jit_solution(3547940520652021247)
XLA Ops:
  9.5 86.3 %gather_inputs.1 = (bf16[8,864,768]{2,1,0:T(8,128)(2,1)}, bf16[8,96,640]{2,1,0:T(8,128)(2,1)}, bf16[4,768,768]{2,1,0:T(8,128)(2,1)}) custom-call(bf16[864,768]{1,0:T(8,128)(2,1)} %pad_maximum_fusion.6.a_ref, bf16[96,640]{1,0:T(8,128)(2,1)} %fusion.22.b_ref, bf16[768,768]{1,0:T(8,128)(2,1)} %t_ref.1), custom_call_target="tpu_custom_call" | custom-call | tf_op jit(solution)/shard_map/gather_inputs/pallas_call | solution.py:282
  97.7 4.6 convolution_convert_fusion.3.kT
  102.4 2.8 fusion.8.qT
  105.2 2.8 fusion.7.vT
  110.4 48.1 %attn_fwd.1 = (f32[192,3072]{1,0:T(8,128)}, bf16[192,3072]{1,0:T(8,128)(2,1)}, f32[3,3072]{1,0:T(4,128)}) custom-call(s32[1,8]{1,0:T(1,128)} %starts.3, bf16[192,3072]{1,0:T(8,128)(2,1)} %fusion.8.qT, bf16[3,3072,64]{2,1,0:T(8,128)(2,1)} %bitcast.127, bf16[192,3072]{1,0:T(8,128)(2,1)} %fusion.7.vT), custom_call_target="tpu_custom_call" | custom-call | tf_op jit(solution)/shard_map/attn_fwd/pallas_call | solution.py:68
  160.9 4.3 all-to-all-start
  166.0 4.8 %slice.159 = bf16[8,384,768]{2,1,0:T(8,128)(2,1)} slice(bf16[8,864,768]{2,1,0:T(8,128)(2,1)} %get-tuple-element.34), slice={[0:8], [480:864], [0:768]} | slice | bytes 9437184 | tf_op jit(solution)/shard_map/slice | solution.py:521
  175.7 4.6 fusion.34
  181.1 3.1 fusion.37
  184.9 31.3 %multiply_convert_fusion = (bf16[768,3072]{1,0:T(8,128)(2,1)}, f32[768,3072]{1,0:T(8,128)}, f32[768,3072]{1,0:T(8,128)}) fusion(f32[3072]{0:T(1024)S(1)} %copy-done.39, bf16[768,768]{1,0:T(8,128)(2,1)S(1)} %bitcast.156, bf16[768,768]{1,0:T(8,128)(2,1)} %bitcast.158, bf16[768,768]{1,0:T(8,128)(2,1)} %bitcast.160, bf16[768,768]{1,0:T(8,128)(2,1)S(1)} %bitcast.154, ...), kind=kOutput, calls=%fused_computation.4 | convolution fusion | flops 3801415680 | bytes 30695424 | tf_op jit(solution)/shard_map/dot_general | solution.py:541
  216.3 6.0 %fusion.38 = (f32[768]{0:T(1024)S(1)}, f32[768,768]{1,0:T(8,128)S(1)}) fusion(f32[768]{0:T(1024)S(1)} %copy-done.43, bf16[768,3072]{1,0:T(8,128)(2,1)} %get-tuple-element.67, bf16[3072,768]{1,0:T(8,128)(2,1)S(1)} %bitcast.143, f32[768]{0:T(1024)S(1)} %get-tuple-element.54, f32[768]{0:T(1024)S(1)} %get-tuple-element.55, f32[768]{0:T(1024)S(1)} %fusion.23, ...), kind=kOutput, calls=%fused_computation.137 | convolution fusion | flops 3628006656 | bytes 14174208 | tf_op jit(solution)/shard_map/dot_general | solution.py:544
  228.0 13.3 %convert_reduce_fusion = (f32[3072]{0:T(1024)}, bf16[768,3072]{1,0:T(8,128)(2,1)}) fusion(f32[768,3072]{1,0:T(8,128)} %get-tuple-element.68, f32[768,3072]{1,0:T(8,128)} %get-tuple-element.112, f32[3072]{0:T(1024)S(1)} %copy-done.39, bf16[768,768]{1,0:T(8,128)(2,1)S(1)} %get-tuple-element.60, bf16[3072,768]{1,0:T(8,128)(2,1)S(1)} %bitcast.144), kind=kOutput, calls=%fused_computation.2 | convolution fusion | flops 3663983616 | bytes 29515776 | tf_op jit(solution)/shard_map/dot_general | solution.py:453
  241.3 8.0 %multiply_reduce_fusion = (f32[768]{0:T(1024)}, f32[768]{0:T(1024)S(1)}, f32[768]{0:T(1024)S(1)}, f32[768,768]{1,0:T(8,128)S(1)}) fusion(f32[768,768]{1,0:T(8,128)S(1)} %get-tuple-element.111, f32[768]{0:T(1024)S(1)} %fusion.23, f32[768]{0:T(1024)S(1)} %broadcast_multiply_fusion.1, f32[768]{0:T(1024)S(1)} %get-tuple-element.55, ...), kind=kOutput, calls=%fused_computation.40 | convolution fusion | flops 3648648960 | bytes 16536576 | tf_op jit(solution)/shard_map/dot_general | solution.py:453
  249.3 6.7 %convolution_convert_fusion.1 = bf16[768,3072]{1,0:T(8,128)(2,1)} fusion(bf16[768,3072]{1,0:T(8,128)(2,1)S(1)} %copy-done.47, f32[768,768]{1,0:T(8,128)S(1)} %get-tuple-element.111, f32[768]{0:T(1024)S(1)} %get-tuple-element.54, f32[768]{0:T(1024)S(1)} %get-tuple-element.55, f32[768]{0:T(1024)S(1)} %fusion.23, f32[768]{0:T(1024)S(1)} %broadcast_multiply_fusion.1), kind=kOutput, calls=%fused_computation.19 | convolution fusion | flops 3629187072 | bytes 11808768 | tf_op jit(solution)/shard_map/dot_general | solution.py:453
  261.7 3.5 all-to-all-start.1
  269.4 2.8 fusion.35
  277.9 4.3 convolution_convert_fusion
  290.2 44.7 %attn_bwd.1 = (bf16[192,3072]{1,0:T(8,128)(2,1)}, bf16[3,3072,64]{2,1,0:T(8,128)(2,1)}, bf16[3,3072,64]{2,1,0:T(8,128)(2,1)}) custom-call(s32[1,8]{1,0:T(1,128)} %starts.3, bf16[192,3072]{1,0:T(8,128)(2,1)} %fusion.8.qT, bf16[3,3072,64]{2,1,0:T(8,128)(2,1)} %bitcast.133, bf16[3,3072,64]{2,1,0:T(8,128)(2,1)} %bitcast.128, bf16[192,3072]{1,0:T(8,128)(2,1)} %copy-done.7, ...), custom_call_target="tpu_custom_call" | custom-call | tf_op jit(solution)/shard_map/attn_bwd/pallas_call | solution.py:129
  334.9 2.8 convert_reduce_fusion.1
  338.5 2.8 copy.92
  343.7 8.2 %convolution_convert_fusion.2 = bf16[3072,768]{1,0:T(8,128)(2,1)} fusion(bf16[192,3072]{1,0:T(8,128)(2,1)} %bitcast.164, bf16[192,3072]{1,0:T(8,128)(2,1)S(1)} %bitcast.162, bf16[192,3072]{1,0:T(8,128)(2,1)} %get-tuple-element.37, bf16[768,640]{1,0:T(8,128)(2,1)} %bitcast.173), kind=kOutput, calls=%fused_computation.20 | convolution fusion | flops 2730885120 | bytes 9240576 | tf_op jit(solution)/shard_map/dot_general | solution.py:453
  352.0 5.3 %fusion.15 = bf16[768,576]{0,1:T(8,128)(2,1)S(1)} fusion(bf16[3072,768]{1,0:T(8,128)(2,1)} %bitcast.187, bf16[192,3072]{1,0:T(8,128)(2,1)S(1)} %bitcast.165, bf16[192,3072]{1,0:T(8,128)(2,1)S(1)} %bitcast.163, bf16[192,3072]{1,0:T(8,128)(2,1)S(1)} %copy-done.13), kind=kOutput, calls=%fused_computation.58 | convolution fusion | flops 2728968192 | bytes 9142272 | tf_op jit(solution)/shard_map/dot_general | solution.py:453
  360.0 100.3 %reduce_grads.1 = (bf16[864,768]{1,0:T(8,128)(2,1)}, bf16[4,96,576]{2,1,0:T(8,128)(2,1)}, bf16[768,768]{1,0:T(8,128)(2,1)}, bf16[768,768]{1,0:T(8,128)(2,1)}, f32[16,128]{1,0:T(8,128)}) custom-call(bf16[4,2,864,768]{3,2,1,0:T(8,128)(2,1)} %constant_dynamic-update-slice_fusion.ga, bf16[4,2,96,576]{3,2,1,0:T(8,128)(2,1)} %bitcast.149, ...), custom_call_target="tpu_custom_call" | custom-call | tf_op jit(solution)/shard_map/reduce_grads/pallas_call | solution.py:424
  466.0 3.4 add_add_fusion.2
  (187 shorter events, 67.0 us)
Async XLA Ops:
  102.3 5.7 %copy-start.7 = (bf16[192,3072]{1,0:T(8,128)(2,1)}, bf16[192,3072]{1,0:T(8,128)(2,1)S(1)}, u32[]{:S(2)}) copy-start(bf16[192,3072]{1,0:T(8,128)(2,1)S(1)} %convolution_convert_fusion.3.kT) | copy-start | bytes 3538948
  160.9 20.2 %all-to-all-start = ((bf16[192,4,768]{2,0,1:T(8,128)(2,1)}), bf16[192,4,768]{2,0,1:T(8,128)(2,1)}, u32[]{:S(2)}, u32[]{:S(2)}) async-start(bf16[192,4,768]{2,0,1:T(8,128)(2,1)} %bitcast.124), calls=%async_computation | async-start | bytes 2359296 | tf_op jit(solution)/shard_map/all_to_all | solution.py:536
  181.1 35.2 %slice-start = ((s8[4718592]{0:T(1024)(128)(4,1)}), s8[4194304]{0:T(1024)(128)(4,1)S(1)}, s32[]{:S(2)}) async-start(s8[4718592]{0:T(1024)(128)(4,1)} %bitcast.141), calls=%async_computation.2 | async-start | bytes 8388608
  184.9 31.4 %slice-start.1 = ((s8[4718592]{0:T(1024)(128)(4,1)}), s8[524288]{0:T(1024)(128)(4,1)S(1)}, s32[]{:S(2)}) async-start(s8[4718592]{0:T(1024)(128)(4,1)} %bitcast.141), calls=%async_computation.3 | async-start | bytes 1048576
  184.9 31.4 %copy-start.43 = (f32[768]{0:T(1024)S(1)}, f32[768]{0:T(1024)}, u32[]{:S(2)}) copy-start(f32[768]{0:T(1024)} %get-tuple-element.53) | copy-start | bytes 9220
  228.0 13.3 %copy-start.9 = (bf16[768,768]{1,0:T(8,128)(2,1)}, bf16[768,768]{1,0:T(8,128)(2,1)S(1)}, u32[]{:S(2)}) copy-start(bf16[768,768]{1,0:T(8,128)(2,1)S(1)} %get-tuple-element.60) | copy-start | bytes 3538948
  228.0 13.3 %copy-start.8 = (bf16[8,96,768]{2,1,0:T(8,128)(2,1)S(1)}, bf16[8,96,768]{2,1,0:T(8,128)(2,1)}, u32[]{:S(2)}) copy-start(bf16[8,96,768]{2,1,0:T(8,128)(2,1)} %get-tuple-element.71) | copy-start | bytes 3538948
  241.3 8.0 %copy-start.47 = (bf16[768,3072]{1,0:T(8,128)(2,1)S(1)}, bf16[768,3072]{1,0:T(8,128)(2,1)}, u32[]{:S(2)}) copy-start(bf16[768,3072]{1,0:T(8,128)(2,1)} %get-tuple-element.58) | copy-start | bytes 14155780
  261.7 5.6 %copy-start.40 = (f32[3072]{0:T(1024)S(1)}, f32[3072]{0:T(1024)}, u32[]{:S(2)}) copy-start(f32[3072]{0:T(1024)} %get-tuple-element.57) | copy-start | bytes 36868
  261.7 5.7 %copy-start.32 = (f32[768]{0:T(1024)S(1)}, f32[768]{0:T(1024)}, u32[]{:S(2)}) copy-start(f32[768]{0:T(1024)} %get-tuple-element.59) | copy-start | bytes 9220
  261.7 6.3 %copy-start.31 = (f32[768]{0:T(1024)S(1)}, f32[768]{0:T(1024)}, u32[]{:S(2)}) copy-start(f32[768]{0:T(1024)} %get-tuple-element.47) | copy-start | bytes 9220
  261.7 7.0 %copy-start.30 = (f32[768]{0:T(1024)S(1)}, f32[768]{0:T(1024)}, u32[]{:S(2)}) copy-start(f32[768]{0:T(1024)} %get-tuple-element.50) | copy-start | bytes 9220
  261.7 23.0 %all-to-all-start.1 = ((bf16[4,192,768]{2,1,0:T(8,128)(2,1)}), bf16[4,192,768]{2,1,0:T(8,128)(2,1)S(1)}, u32[]{:S(2)}, u32[]{:S(2)}) async-start(bf16[4,192,768]{2,1,0:T(8,128)(2,1)} %bitcast.41), calls=%async_computation.1 | async-start | bytes 2359296 | tf_op jit(solution)/shard_map/all_to_all | solution.py:560
  269.4 8.5 %slice-start.2 = ((s8[4718592]{0:T(1024)(128)(4,1)}), s8[4194304]{0:T(1024)(128)(4,1)S(1)}, s32[]{:S(2)}) async-start(s8[4718592]{0:T(1024)(128)(4,1)} %bitcast.190), calls=%async_computation.4 | async-start | bytes 8388608
  272.2 5.7 %slice-start.3 = ((s8[4718592]{0:T(1024)(128)(4,1)}), s8[524288]{0:T(1024)(128)(4,1)S(1)}, s32[]{:S(2)}) async-start(s8[4718592]{0:T(1024)(128)(4,1)} %bitcast.190), calls=%async_computation.5 | async-start | bytes 1048576
  343.7 8.2 %copy-start.11 = (bf16[3,64,3072]{2,1,0:T(8,128)(2,1)S(1)}, bf16[3,64,3072]{2,1,0:T(8,128)(2,1)}, u32[]{:S(2)}) copy-start(bf16[3,64,3072]{2,1,0:T(8,128)(2,1)} %copy.93) | copy-start | bytes 3538948
  343.7 8.2 %copy-start.13 = (bf16[192,3072]{1,0:T(8,128)(2,1)S(1)}, bf16[192,3072]{1,0:T(8,128)(2,1)}, u32[]{:S(2)}) copy-start(bf16[192,3072]{1,0:T(8,128)(2,1)} %get-tuple-element.37) | copy-start | bytes 3538948
  351.9 5.7 %copy-start.45 = (f32[192]{0:T(256)S(1)}, f32[192]{0:T(256)}, u32[]{:S(2)}) copy-start(f32[192]{0:T(256)} %convert_reduce_fusion.5) | copy-start | bytes 2308
  351.9 7.4 %copy-start.33 = (f32[8,1,96]{2,1,0:T(1,128)S(1)}, f32[8,1,96]{2,1,0:T(1,128)}, u32[]{:S(2)}) copy-start(f32[8,1,96]{2,1,0:T(1,128)} %stack_reshape.26) | copy-start | bytes 9220
  351.9 7.3 %copy-start.34 = (f32[8,1,96]{2,1,0:T(1,128)S(1)}, f32[8,1,96]{2,1,0:T(1,128)}, u32[]{:S(2)}) copy-start(f32[8,1,96]{2,1,0:T(1,128)} %stack_reshape.28) | copy-start | bytes 9220
  352.0 7.3 %copy-start.35 = (f32[8,1,96]{2,1,0:T(1,128)S(1)}, f32[8,1,96]{2,1,0:T(1,128)}, u32[]{:S(2)}) copy-start(f32[8,1,96]{2,1,0:T(1,128)} %stack_reshape.29) | copy-start | bytes 9220
  352.0 7.3 %copy-start.36 = (f32[8,1,96]{2,1,0:T(1,128)S(1)}, f32[8,1,96]{2,1,0:T(1,128)}, u32[]{:S(2)}) copy-start(f32[8,1,96]{2,1,0:T(1,128)} %stack_reshape.27) | copy-start | bytes 9220
  352.0 7.3 %copy-start.37 = (f32[8,1,96]{2,1,0:T(1,128)S(1)}, f32[8,1,96]{2,1,0:T(1,128)}, u32[]{:S(2)}) copy-start(f32[8,1,96]{2,1,0:T(1,128)} %stack_reshape.30) | copy-start | bytes 9220
  352.0 7.3 %copy-start.38 = (f32[8,1,96]{2,1,0:T(1,128)S(1)}, f32[8,1,96]{2,1,0:T(1,128)}, u32[]{:S(2)}) copy-start(f32[8,1,96]{2,1,0:T(1,128)} %stack_reshape.31) | copy-start | bytes 9220
  (30 other events, 80.5 us)

commit v3 on v2

--- a/solution.py
+++ b/solution.py
@@ -438,6 +438,164 @@
     )(ga.reshape((4, 2) + ga.shape[1:]), gb.reshape((4, 2) + gb.shape[1:]), dx.reshape((2, 2) + dx.shape[1:]), sm.reshape((4, 2) + sm.shape[1:]))
 
 
+def mm(a, b, left, right):
+    return lax.dot_general(a, b, (((left,), (right,)), ((), ())), preferred_element_type=f32)
+
+
+def chunks(total, step, body):
+    def run(i, _):
+        body(pl.ds(pl.multiple_of(i * step, step), step))
+        return 0
+    lax.fori_loop(0, total // step, run, 0)
+
+
+def ffn_kernel(n, r, step, mixed, tokens, cot, vec, big, out, dres, ga, dO, small,
+               w_out, w_in, w_outer, stage, fb, gp, xh1, n1b, dh2, dm, du, acc, r1, lsem, gsem):
+    toks, model = tokens.shape
+    wide = w_in.shape[0]
+    per = n // wide
+    def outer_at(ref, j):
+        if per:
+            return ref.at[pl.ds(j * per, per), pl.ds((1 + wide) * r, wide * r)]
+        return ref.at[:, pl.ds((1 + wide + j) * r, r)]
+    loads = [pltpu.make_async_copy(big.at[:, pl.ds(0, r)], w_out, lsem.at[0])]
+    for j in range(wide):
+        loads.append(pltpu.make_async_copy(big.at[:, pl.ds((1 + j) * r, r)], w_in.at[j], lsem.at[1 + j]))
+    for j in range(wide):
+        loads.append(pltpu.make_async_copy(outer_at(big, j), w_outer.at[j], lsem.at[1 + wide + j]))
+    for load in loads:
+        load.start()
+    stores = []
+
+    def put(value_rows, place):
+        k = len(stores)
+        slot = k % stage.shape[0]
+        if k >= stage.shape[0]:
+            stores[k - stage.shape[0]].wait()
+        def body(at):
+            stage[slot, at, :] = value_rows(at).astype(bf)
+        chunks(model, step, body)
+        shape = place.shape
+        store = pltpu.make_async_copy(stage.at[slot].reshape(shape), place, gsem.at[slot])
+        store.start()
+        stores.append(store)
+
+    flat = lambda ref: ref.reshape(model, model)
+    row = lambda i: vec[i:i + 1, :]
+    b_output, b_outer, g1, s1, g2, s2 = [row(i) for i in (2, 3, 4, 5, 6, 7)]
+    small[...] = jnp.zeros_like(small)
+    loads[0].wait()
+    wo = flat(w_out)
+
+    def first(at):
+        attn = mm(mixed[:, at], wo[...], 0, 0)
+        z = tokens[at, :].astype(f32) + (attn + b_output)
+        cen = z - jnp.mean(z, axis=-1, keepdims=True)
+        inv = lax.rsqrt(jnp.mean(cen * cen, axis=-1, keepdims=True) + NORM_EPS)
+        xh = cen * inv
+        norm = xh * g1 + s1
+        xh1[at, :] = xh
+        n1b[at, :] = norm.astype(bf)
+        r1[at, :] = jnp.broadcast_to(inv, (inv.shape[0], 128))
+        acc[at, :] = norm + b_outer
+    chunks(toks, step, first)
+    for j in range(wide):
+        loads[1 + j].wait()
+        wi = flat(w_in.at[j])
+        bias = row(8 + j)
+        def inner(at, j=j, wi=wi, bias=bias):
+            u = mm(n1b[at, :], wi[...], 1, 0) + bias
+            cdf = 0.5 * (1.0 + lax.erf(u * (0.5 ** 0.5)))
+            pdf = jnp.exp(-0.5 * u * u) * 0.3989422804014327
+            fb[j, at, :] = (u * cdf).astype(bf)
+            gp[j, at, :] = cdf + u * pdf
+        chunks(toks, step, inner)
+        loads[1 + wide + j].wait()
+        wout = flat(w_outer.at[j])
+        def outer(at, j=j, wout=wout):
+            acc[at, :] += mm(fb[j, at, :], wout[...], 1, 0)
+        chunks(toks, step, outer)
+
+    def second(at):
+        z = acc[at, :]
+        cen = z - jnp.mean(z, axis=-1, keepdims=True)
+        inv = lax.rsqrt(jnp.mean(cen * cen, axis=-1, keepdims=True) + NORM_EPS)
+        xh = cen * inv
+        out[at, :] = (xh * g2 + s2).astype(bf)
+        g = cot[at, :].astype(f32)
+        gx = g * xh
+        gh = g * g2
+        d = inv * (gh - jnp.mean(gh, axis=-1, keepdims=True) - xh * jnp.mean(gh * xh, axis=-1, keepdims=True))
+        dh2[at, :] = d
+        low = d.astype(bf)
+        dm[at, :] = low
+        small[6:7, :] += jnp.sum(gx, axis=0, keepdims=True)
+        small[7:8, :] += jnp.sum(g, axis=0, keepdims=True)
+        small[3:4, :] += jnp.sum(low.astype(f32), axis=0, keepdims=True)
+    chunks(toks, step, second)
+    for j in range(wide):
+        wout = flat(w_outer.at[j])
+        put(lambda at, j=j: mm(fb[j, :, at], dm[...], 0, 0), outer_at(ga, j))
+        def dinner(at, j=j, wout=wout):
+            low = (gp[j, at, :] * mm(dm[at, :], wout[...], 1, 1)).astype(bf)
+            du[at, :] = low
+            small[8 + j:9 + j, :] += jnp.sum(low.astype(f32), axis=0, keepdims=True)
+        chunks(toks, step, dinner)
+        wi = flat(w_in.at[j])
+        def dfirst(at, wi=wi):
+            dh2[at, :] += mm(du[at, :], wi[...], 1, 1)
+        chunks(toks, step, dfirst)
+        put(lambda at: mm(n1b[:, at], du[...], 0, 0), ga.at[:, pl.ds((1 + j) * r, r)])
+
+    def last(at):
+        d = dh2[at, :]
+        xh = xh1[at, :]
+        gh = d * g1
+        inv = r1[at, 0:1]
+        z = inv * (gh - jnp.mean(gh, axis=-1, keepdims=True) - xh * jnp.mean(gh * xh, axis=-1, keepdims=True))
+        dres[at, :] = z
+        low = z.astype(bf)
+        dm[at, :] = low
+        small[4:5, :] += jnp.sum(d * xh, axis=0, keepdims=True)
+        small[5:6, :] += jnp.sum(d, axis=0, keepdims=True)
+        small[2:3, :] += jnp.sum(low.astype(f32), axis=0, keepdims=True)
+    chunks(toks, step, last)
+
+    def back(at):
+        dO[at, :] = mm(wo[at, :], dm[...], 1, 1).astype(bf)
+    chunks(model, step, back)
+    put(lambda at: mm(mixed[at, :], dm[...], 1, 0), ga.at[:, pl.ds(0, r)])
+    for store in stores[-stage.shape[0]:]:
+        store.wait()
+
+
+def ffn_block(mixed, tokens, cot, vec, big, step=384):
+    n, rows9, model = big.shape
+    r = model // n
+    wide = (rows9 // r - 1) // 2
+    toks = tokens.shape[0]
+    vmem = pl.BlockSpec(memory_space=pltpu.VMEM)
+    hbm = pl.BlockSpec(memory_space=pl.ANY)
+    per = n // wide
+    ohold = (per, wide * r, model) if per else (n, r, model)
+    V = pltpu.VMEM
+    sq = lambda dt, *lead: V(lead + (toks, model), dt)
+    return pl.pallas_call(
+        functools.partial(ffn_kernel, n, r, step),
+        in_specs=[vmem] * 4 + [hbm],
+        out_specs=[vmem, vmem, hbm, vmem, vmem],
+        out_shape=[jax.ShapeDtypeStruct((toks, model), bf), jax.ShapeDtypeStruct((toks, model), f32),
+                   jax.ShapeDtypeStruct(big.shape, bf), jax.ShapeDtypeStruct((model, toks), bf),
+                   jax.ShapeDtypeStruct((16, model), f32)],
+        scratch_shapes=[V((n, r, model), bf), V((wide, n, r, model), bf), V((wide,) + ohold, bf), V((4, model, model), bf),
+                        sq(bf, wide), sq(f32, wide), sq(f32), sq(bf), sq(f32), sq(bf), sq(bf), sq(f32),
+                        V((toks, 128), f32), pltpu.SemaphoreType.DMA((1 + 2 * wide,)), pltpu.SemaphoreType.DMA((4,))],
+        compiler_params=pltpu.CompilerParams(vmem_limit_bytes=67043328),
+        cost_estimate=pl.CostEstimate(flops=2 * toks * model * model * (3 + 6 * wide), bytes_accessed=4 * big.size, transcendentals=2 * toks * model * wide),
+        name="ffn_block",
+    )(mixed, tokens, cot, vec, big)
+
+
 def layer_norm(inputs, norm_gain, norm_bias):
     row_mean = jnp.mean(inputs, axis=-1, keepdims=True)
     centred = inputs - row_mean
@@ -482,58 +640,17 @@
     )
 
 
-def shards(
-    tokens, cotangent, starts,
-    w_query, w_key, w_value, w_output, w_inner, w_outer,
-    b_query, b_value, b_output, b_inner, b_outer,
-    gain_first, bias_first, gain_second, bias_second,
-):
-    model = tokens.shape[1]
-    rows = w_query.shape[0]
-    shards_n = lax.axis_size("wshard")
-    seq_n = lax.axis_size("seq")
-    seq_i = lax.axis_index("seq")
-    width = model // seq_n
-    heads = width // HD
-    wide = w_inner.shape[1] // model
-
-    def own(columns):
-        return lax.dynamic_slice_in_dim(columns, seq_i * width, width, columns.ndim - 1)
-
-    smalls = (b_query, b_value, b_output, b_outer, gain_first, bias_first, gain_second, bias_second)
-    small_cols = jnp.stack(smalls + tuple(b_inner.reshape(wide, rows)), axis=1)
-    cols_n = small_cols.shape[1]
-    a = jnp.concatenate(
-        [w_output, w_inner.reshape(rows, wide, model).transpose(1, 0, 2).reshape(wide * rows, model), w_outer], axis=0
-    )
-    b = jnp.concatenate([own(w_query), own(w_key), own(w_value), jnp.pad(small_cols, ((0, 0), (0, HD - cols_n)))], axis=1)
-    big, side, stream = gather_parts(a, b, tokens)
-    stream = stream.reshape(-1, model)
-    side = side.reshape(model, -1)
-    w_own = side[:, :3 * width]
-    vectors = side[:, 3 * width:3 * width + cols_n].astype(f32).T
-    bias_query, bias_value, bias_output, bias_outer, gain_one, shift_one, gain_two, shift_two = vectors[:8]
-    bias_inner = vectors[8:].reshape(wide, shards_n, rows).transpose(1, 0, 2).reshape(-1)
+def ffn_plain(mixed, tokens, cotangent, vec, big):
+    shards_n, rows9, model = big.shape
+    rows = model // shards_n
+    wide = (rows9 // rows - 1) // 2
+    bias_output, bias_outer, gain_one, shift_one, gain_two, shift_two = vec[2:8]
+    bias_inner = vec[8:8 + wide].reshape(-1)
     output_full = big[:, :rows].reshape(model, model)
     inner_full = jnp.concatenate(
         [big[:, (1 + j) * rows:(2 + j) * rows].reshape(model, model) for j in range(wide)], axis=1
     )
     outer_full = big[:, (1 + wide) * rows:].reshape(-1, model)
-
-    scale = HD ** -0.5
-    qT = ((contract(w_own[:, :width], stream, 0, 1) + own(bias_query)[:, None]).astype(bf) * bf(scale))
-    kT = contract(w_own[:, width:2 * width], stream, 0, 1).astype(bf)
-    vT = (contract(w_own[:, 2 * width:], stream, 0, 1) + own(bias_value)[:, None]).astype(bf)
-
-    def by_token(arr):
-        return arr.reshape(heads, HD, -1).transpose(0, 2, 1)
-
-    def by_feature(arr):
-        return arr.transpose(0, 2, 1).reshape(width, -1)
-
-    q3, k3, v3 = by_token(qT), by_token(kT), by_token(vT)
-    oT, mixT, lse = attn_fwd(starts, qT, k3, vT, 512, 512)
-    mixed = lax.all_to_all(mixT, "seq", split_axis=1, concat_axis=0, tiled=True)
 
     residual_in = tokens.astype(f32) + contract(mixed, output_full, 0, 0) + bias_output
     first_norm, first_back = jax.vjp(layer_norm, residual_in, gain_one, shift_one)
@@ -557,29 +674,85 @@
     grad_bias_output = jnp.sum(d_attn.astype(f32), axis=0)
     grad_output = contract(mixed, d_attn, 1, 0)
     d_mixed = contract(output_full, d_attn, 1, 1).astype(bf)
+    by_rows = lambda grad: grad.astype(bf).reshape(shards_n, -1, model)
+    ga = jnp.concatenate(
+        [by_rows(grad_output)] + [by_rows(grad_inner[:, j * model:(j + 1) * model]) for j in range(wide)]
+        + [by_rows(grad_outer)], axis=1,
+    )
+    none = jnp.zeros((model,), f32)
+    sums = jnp.concatenate([
+        jnp.stack([none, none, grad_bias_output, grad_bias_outer, grad_gain_one, grad_bias_one, grad_gain_two, grad_bias_two]),
+        grad_bias_inner.reshape(wide, model)], axis=0)
+    return layer_result.astype(bf), d_resid, ga, d_mixed, sums
+
+
+def shards(
+    tokens, cotangent, starts,
+    w_query, w_key, w_value, w_output, w_inner, w_outer,
+    b_query, b_value, b_output, b_inner, b_outer,
+    gain_first, bias_first, gain_second, bias_second,
+):
+    model = tokens.shape[1]
+    rows = w_query.shape[0]
+    shards_n = lax.axis_size("wshard")
+    seq_n = lax.axis_size("seq")
+    seq_i = lax.axis_index("seq")
+    width = model // seq_n
+    heads = width // HD
+    wide = w_inner.shape[1] // model
+
+    def own(columns):
+        return lax.dynamic_slice_in_dim(columns, seq_i * width, width, columns.ndim - 1)
+
+    smalls = (b_query, b_value, b_output, b_outer, gain_first, bias_first, gain_second, bias_second)
+    small_cols = jnp.stack(smalls + tuple(b_inner.reshape(wide, rows)), axis=1)
+    cols_n = small_cols.shape[1]
+    a = jnp.concatenate(
+        [w_output, w_inner.reshape(rows, wide, model).transpose(1, 0, 2).reshape(wide * rows, model), w_outer], axis=0
+    )
+    b = jnp.concatenate([own(w_query), own(w_key), own(w_value), jnp.pad(small_cols, ((0, 0), (0, HD - cols_n)))], axis=1)
+    big, side, stream = gather_parts(a, b, tokens)
+    stream = stream.reshape(-1, model)
+    side = side.reshape(model, -1)
+    w_own = side[:, :3 * width]
+    vectors = side[:, 3 * width:3 * width + cols_n].astype(f32).T
+    bias_query, bias_value = vectors[:2]
+    bias_inner = vectors[8:].reshape(wide, shards_n, rows).transpose(1, 0, 2).reshape(-1)
+    scale = HD ** -0.5
+    qT = ((contract(w_own[:, :width], stream, 0, 1) + own(bias_query)[:, None]).astype(bf) * bf(scale))
+    kT = contract(w_own[:, width:2 * width], stream, 0, 1).astype(bf)
+    vT = (contract(w_own[:, 2 * width:], stream, 0, 1) + own(bias_value)[:, None]).astype(bf)
+
+    def by_token(arr):
+        return arr.reshape(heads, HD, -1).transpose(0, 2, 1)
+
+    def by_feature(arr):
+        return arr.transpose(0, 2, 1).reshape(width, -1)
+
+    q3, k3, v3 = by_token(qT), by_token(kT), by_token(vT)
+    oT, mixT, lse = attn_fwd(starts, qT, k3, vT, 512, 512)
+    mixed = lax.all_to_all(mixT, "seq", split_axis=1, concat_axis=0, tiled=True)
+
+    vec = jnp.concatenate([vectors[:8], bias_inner.reshape(wide, model), jnp.zeros((4, model), f32)], axis=0)
+    feed = ffn_block if chips_of_two_by_four() else ffn_plain
+    layer_result, d_resid, ga, d_mixed, sums = feed(mixed, tokens, cotangent, vec, big)
     doT = lax.all_to_all(d_mixed, "seq", split_axis=0, concat_axis=1, tiled=True)
 
     dqT, dk3, dv3 = attn_bwd(starts, qT, q3, k3, kT, v3, doT, by_token(doT), oT, lse, 256, 512)
     dT = jnp.concatenate([dqT, by_feature(dk3), by_feature(dv3)], axis=0)
     gb = contract(stream, dT, 0, 1).astype(bf).reshape(shards_n, rows, -1)
     dx = contract(dT, w_own, 0, 1).astype(bf).reshape(seq_n, -1, model)
-    by_rows = lambda grad: grad.astype(bf).reshape(shards_n, -1, model)
-    ga = jnp.concatenate(
-        [by_rows(grad_output)] + [by_rows(grad_inner[:, j * model:(j + 1) * model]) for j in range(wide)]
-        + [by_rows(grad_outer)], axis=1,
-    )
-
     def spread(own_sum):
         return lax.dynamic_update_slice(jnp.zeros((model,), f32), own_sum, (seq_i * width,))
 
     small_rows = (
         spread(jnp.sum(dqT.astype(f32), axis=1)),
         spread(jnp.sum(dv3.astype(f32), axis=1).reshape(-1)),
-        grad_bias_output, grad_bias_outer, grad_gain_one, grad_bias_one, grad_gain_two, grad_bias_two,
+        *sums[2:8],
     )
     sm = jnp.concatenate(
         [jnp.stack([row.reshape(shards_n, rows) for row in small_rows], axis=1),
-         grad_bias_inner.reshape(shards_n, wide, rows)], axis=1,
+         sums[8:8 + wide].reshape(shards_n, wide, rows)], axis=1,
     )
     sm = jnp.pad(sm, ((0, 0), (0, -cols_n % 8), (0, -rows % 128)))
     fa, fb, fx, fr, fs = reduce_parts(ga, gb, dx, sm)
@@ -593,7 +766,7 @@
     tail = [fs[i, :rows] for i in range(8)]
     g_b_inner = fs[8:8 + wide, :rows].reshape(-1)
     return (
-        layer_result.astype(bf), d_tokens, *grads,
+        layer_result, d_tokens, *grads,
         fa[:rows], g_inner, fa[(1 + wide) * rows:],
         tail[0], tail[1], tail[2], g_b_inner, *tail[3:],
     )

time: 481 us -> 455 us (0.946); the launches traced: 473 us -> 460 us
  matrix products: 101 us -> 23.7 us
  Pallas kernels: 279 us -> 351 us
  local copies, waits for them, and re-layouts: 62.8 us -> 40.1 us
  waiting for transfers between devices: 0.82 us -> 21.7 us
  other arithmetic: 20.2 us -> 14.4 us
    pallas_call x0 -> x1, Pallas kernels: none -> 60.9 us  [ffn_block(): pl.pallas_call(functools.partial(ffn_kernel, n, r, step), in_specs=[vmem]...]
    dot_general x12 -> x5, matrix products: 63.5 us -> 23.7 us  [contract(): lax.dot_general(left_in, right_in, (((left_dim,), (right_dim,)), ((), ())...]
    dot_general x2 -> x0, matrix products: 37.4 us -> none  [the longest x1 31.3 us: shards(): jnp.dot(first_low, inner_full, preferred_element_type=f32) + bias_inner]
    all_to_all x1, waiting for transfers between devices: 0.82 us -> 14.9 us  [shards(): mixed = lax.all_to_all(mixT, 'seq', split_axis=1, concat_axis=0, tiled=True)]
    slice x3 -> x2, local copies, waits for them, and re-layouts: 12.2 us -> 0.01 us  [the longest x1 0.01 us: shards(): vectors[:8]]
    pallas_call x1, Pallas kernels: 100 us -> 108 us  [reduce_grads(): pl.pallas_call(reduce_kernel, in_specs=[vmem] * 4, out_specs=[vmem] * 5,...]
    unnamed x110 -> x69, local copies, waits for them, and re-layouts: 7.13 us -> 0.27 us
    all_to_all x1, waiting for transfers between devices: 0.01 us -> 6.77 us  [shards(): lax.all_to_all(d_mixed, 'seq', split_axis=0, concat_axis=1, tiled=True)]
  transfers between devices with their start and end apart: 2 -> 2, of which waited for: 1 -> 2; matrix products, arithmetic and copies ran while one was open for 7% -> 2% of each run, Pallas kernels for 0% -> 0%
where the time goes in v3:
time: 455 us; the launch traced here: 460 us
  Pallas kernels  351 us (77%)
  local copies, waits for them, and re-layouts  40.1 us (9%)
  matrix products  23.7 us (5%)
  waiting for transfers between devices  21.7 us (5%)
  other arithmetic  14.4 us (3%)
  starting transfers between devices  8.2 us (2%)
    pallas_call x1, Pallas kernels, reduce_grads(): pl.pallas_call(reduce_kernel, in_specs=[vmem] * 4, out_specs=[vmem] * 5,...  108 us
    pallas_call x1, Pallas kernels, gather_inputs(): pl.pallas_call(gather_kernel, in_specs=[vmem] * 3, out_specs=[hbm] * 3, o...  86.3 us
    pallas_call x1, Pallas kernels, ffn_block(): pl.pallas_call(functools.partial(ffn_kernel, n, r, step), in_specs=[vmem]...  60.9 us
    pallas_call x1, Pallas kernels, attn_fwd(): pl.pallas_call(functools.partial(fwd_kernel, heads, bq, bk), grid=(total...  48.2 us
    pallas_call x1, Pallas kernels, attn_bwd(): pl.pallas_call(functools.partial(bwd_kernel, heads, bq, bk), grid=(total...  48.1 us
    dot_general x5, matrix products, contract(): lax.dot_general(left_in, right_in, (((left_dim,), (right_dim,)), ((), ())...  23.7 us
    all_to_all x1, waiting for transfers between devices, shards(): mixed = lax.all_to_all(mixT, 'seq', split_axis=1, concat_axis=0, tiled=True)  14.9 us
    reshape x5, local copies, waits for them, and re-layouts, by_token(): return arr.reshape(heads, HD, -1).transpose(0, 2, 1)  10.6 us
  transfers between devices with their start and end apart: 2, of which 2 were waited for; matrix products, arithmetic and copies ran while one was open for 2% of the time, Pallas kernels for 0%

profile of v3, /device:TPU:0, one launch (start us, length us, event | category | flops | bytes accessed | tf_op | source)
XLA Modules:
  0.0 460.3 jit_solution(14693933951411821051)
XLA Ops:
  6.6 2.2 pad_maximum_fusion.5.a_ref
  9.5 86.3 %gather_inputs.1 = (bf16[8,864,768]{2,1,0:T(8,128)(2,1)}, bf16[8,96,640]{2,1,0:T(8,128)(2,1)}, bf16[4,768,768]{2,1,0:T(8,128)(2,1)}) custom-call(bf16[864,768]{1,0:T(8,128)(2,1)} %pad_maximum_fusion.5.a_ref, bf16[96,640]{1,0:T(8,128)(2,1)} %fusion.10.b_ref, bf16[768,768]{1,0:T(8,128)(2,1)} %tokens.1), custom_call_target="tpu_custom_call" | custom-call | tf_op jit(solution)/shard_map/gather_inputs/pallas_call | solution.py:282
  97.1 4.6 %convolution_convert_fusion.1.kT = bf16[192,3072]{1,0:T(8,128)(2,1)S(1)} fusion(bf16[3072,768]{1,0:T(8,128)(2,1)} %bitcast.155, bf16[768,640]{1,0:T(8,128)(2,1)} %bitcast.135), kind=kOutput, calls=%fused_computation.6 | convolution fusion | flops 906559488 | bytes 6291456 | tf_op jit(solution)/shard_map/dot_general | solution.py:611
  101.8 2.8 fusion.1.vT
  104.6 2.8 fusion.2.qT
  107.4 2.4 copy.93
  109.8 48.2 %attn_fwd.1 = (f32[192,3072]{1,0:T(8,128)}, bf16[192,3072]{1,0:T(8,128)(2,1)}, f32[3,3072]{1,0:T(4,128)}) custom-call(s32[1,8]{1,0:T(1,128)} %starts.3, bf16[192,3072]{1,0:T(8,128)(2,1)} %fusion.2.qT, bf16[3,3072,64]{2,1,0:T(8,128)(2,1)} %bitcast.108, bf16[192,3072]{1,0:T(8,128)(2,1)} %fusion.1.vT), custom_call_target="tpu_custom_call" | custom-call | tf_op jit(solution)/shard_map/attn_fwd/pallas_call | solution.py:68
  157.9 2.4 copy.117
  160.3 4.5 all-to-all-start
  165.8 14.9 %all-to-all-done = bf16[192,4,768]{2,0,1:T(8,128)(2,1)} async-done(((bf16[192,4,768]{2,0,1:T(8,128)(2,1)}), bf16[192,4,768]{2,0,1:T(8,128)(2,1)}, u32[]{:S(2)}, u32[]{:S(2)}) %all-to-all-start) | async-done | bytes 1179680 | tf_op jit(solution)/shard_map/all_to_all | solution.py:734
  180.7 60.9 %ffn_block.1 = (bf16[768,768]{1,0:T(8,128)(2,1)}, f32[768,768]{1,0:T(8,128)}, bf16[8,864,768]{2,1,0:T(8,128)(2,1)}, bf16[768,768]{1,0:T(8,128)(2,1)}, f32[16,768]{1,0:T(8,128)}) custom-call(bf16[768,768]{1,0:T(8,128)(2,1)} %bitcast.22.mixed, bf16[768,768]{1,0:T(8,128)(2,1)} %tokens.1, bf16[768,768]{1,0:T(8,128)(2,1)} %cot.1, ...), custom_call_target="tpu_custom_call" | custom-call | flops 24461180928 | bytes 21233664 | tf_op jit(solution)/shard_map/ffn_block/pallas_call | solution.py:583
  241.6 3.7 all-to-all-start.1
  245.3 2.4 copy.97
  247.8 2.4 copy.96
  254.4 6.8 %all-to-all-done.1 = bf16[4,192,768]{2,1,0:T(8,128)(2,1)S(1)} async-done(((bf16[4,192,768]{2,1,0:T(8,128)(2,1)}), bf16[4,192,768]{2,1,0:T(8,128)(2,1)S(1)}, u32[]{:S(2)}, u32[]{:S(2)}) %all-to-all-start.1) | async-done | bytes 1179680 | tf_op jit(solution)/shard_map/all_to_all | solution.py:739
  262.9 2.5 copy.100
  266.6 48.1 %attn_bwd.1 = (bf16[192,3072]{1,0:T(8,128)(2,1)}, bf16[3,3072,64]{2,1,0:T(8,128)(2,1)}, bf16[3,3072,64]{2,1,0:T(8,128)(2,1)}) custom-call(s32[1,8]{1,0:T(1,128)} %starts.3, bf16[192,3072]{1,0:T(8,128)(2,1)} %fusion.2.qT, bf16[3,3072,64]{2,1,0:T(8,128)(2,1)} %bitcast.116, bf16[3,3072,64]{2,1,0:T(8,128)(2,1)} %bitcast.109, bf16[192,3072]{1,0:T(8,128)(2,1)} %copy-done.4, ...), custom_call_target="tpu_custom_call" | custom-call | tf_op jit(solution)/shard_map/attn_bwd/pallas_call | solution.py:129
  314.6 2.8 convert_reduce_fusion
  318.3 2.8 copy.101
  323.2 8.2 %convolution_convert_fusion = bf16[3072,768]{1,0:T(8,128)(2,1)} fusion(bf16[192,3072]{1,0:T(8,128)(2,1)} %bitcast.127, bf16[192,3072]{1,0:T(8,128)(2,1)S(1)} %bitcast.125, bf16[192,3072]{1,0:T(8,128)(2,1)} %get-tuple-element.45, bf16[768,640]{1,0:T(8,128)(2,1)} %bitcast.136), kind=kOutput, calls=%fused_computation | convolution fusion | flops 2730885120 | bytes 9240576 | tf_op jit(solution)/shard_map/dot_general | solution.py:611
  331.5 5.3 %fusion.4 = bf16[768,576]{0,1:T(8,128)(2,1)S(1)} fusion(bf16[3072,768]{1,0:T(8,128)(2,1)} %bitcast.156, bf16[192,3072]{1,0:T(8,128)(2,1)S(1)} %bitcast.128, bf16[192,3072]{1,0:T(8,128)(2,1)S(1)} %bitcast.126, bf16[192,3072]{1,0:T(8,128)(2,1)S(1)} %copy-done.8), kind=kOutput, calls=%fused_computation.12 | convolution fusion | flops 2728968192 | bytes 9142272 | tf_op jit(solution)/shard_map/dot_general | solution.py:611
  339.8 107.5 %reduce_grads.1 = (bf16[864,768]{1,0:T(8,128)(2,1)}, bf16[4,96,576]{2,1,0:T(8,128)(2,1)}, bf16[768,768]{1,0:T(8,128)(2,1)}, bf16[768,768]{1,0:T(8,128)(2,1)}, f32[16,128]{1,0:T(8,128)}) custom-call(bf16[4,2,864,768]{3,2,1,0:T(8,128)(2,1)} %bitcast.112, bf16[4,2,96,576]{3,2,1,0:T(8,128)(2,1)} %bitcast.122, bf16[2,2,768,768]{3,2,1,0:T(8,128)(2,1)} %bitcast.119, ...), custom_call_target="tpu_custom_call" | custom-call | tf_op jit(solution)/shard_map/reduce_grads/pallas_call | solution.py:424
  447.4 2.2 fusion.13
  453.0 3.3 add_add_fusion
  (123 shorter events, 29.1 us)
Async XLA Ops:
  97.0 4.8 %copy-start.22 = (bf16[8,96,640]{2,1,0:T(8,128)(2,1)S(1)}, bf16[8,96,640]{2,1,0:T(8,128)(2,1)}, u32[]{:S(2)}) copy-start(bf16[8,96,640]{2,1,0:T(8,128)(2,1)} %get-tuple-element.36) | copy-start | bytes 2949124
  97.0 4.7 %copy-start.33 = (bf16[4,768,768]{2,1,0:T(8,128)(2,1)S(1)}, bf16[4,768,768]{2,1,0:T(8,128)(2,1)}, u32[]{:S(2)}) copy-start(bf16[4,768,768]{2,1,0:T(8,128)(2,1)} %get-tuple-element.37) | copy-start | bytes 14155780
  101.7 5.7 %copy-start.4 = (bf16[192,3072]{1,0:T(8,128)(2,1)}, bf16[192,3072]{1,0:T(8,128)(2,1)S(1)}, u32[]{:S(2)}) copy-start(bf16[192,3072]{1,0:T(8,128)(2,1)S(1)} %convolution_convert_fusion.1.kT) | copy-start | bytes 3538948
  160.3 20.4 %all-to-all-start = ((bf16[192,4,768]{2,0,1:T(8,128)(2,1)}), bf16[192,4,768]{2,0,1:T(8,128)(2,1)}, u32[]{:S(2)}, u32[]{:S(2)}) async-start(bf16[192,4,768]{2,0,1:T(8,128)(2,1)} %bitcast.105), calls=%async_computation | async-start | bytes 2359296 | tf_op jit(solution)/shard_map/all_to_all | solution.py:734
  241.6 3.7 copy-start.3
  241.6 19.5 %all-to-all-start.1 = ((bf16[4,192,768]{2,1,0:T(8,128)(2,1)}), bf16[4,192,768]{2,1,0:T(8,128)(2,1)S(1)}, u32[]{:S(2)}, u32[]{:S(2)}) async-start(bf16[4,192,768]{2,1,0:T(8,128)(2,1)} %bitcast.129), calls=%async_computation.1 | async-start | bytes 2359296 | tf_op jit(solution)/shard_map/all_to_all | solution.py:739
  314.6 2.8 copy-start.7
  317.4 3.6 copy-start.1
  323.2 8.2 %copy-start.6 = (bf16[3,64,3072]{2,1,0:T(8,128)(2,1)S(1)}, bf16[3,64,3072]{2,1,0:T(8,128)(2,1)}, u32[]{:S(2)}) copy-start(bf16[3,64,3072]{2,1,0:T(8,128)(2,1)} %copy.102) | copy-start | bytes 3538948
  323.2 8.2 %copy-start.8 = (bf16[192,3072]{1,0:T(8,128)(2,1)S(1)}, bf16[192,3072]{1,0:T(8,128)(2,1)}, u32[]{:S(2)}) copy-start(bf16[192,3072]{1,0:T(8,128)(2,1)} %get-tuple-element.45) | copy-start | bytes 3538948
  331.4 5.3 %copy-start.30 = (f32[3,64]{1,0:T(4,128)S(1)}, f32[3,64]{1,0:T(4,128)}, u32[]{:S(2)}) copy-start(f32[3,64]{1,0:T(4,128)} %convert_reduce_fusion) | copy-start | bytes 2308
  331.4 6.0 %copy-start.32 = (f32[192]{0:T(256)S(1)}, f32[192]{0:T(256)}, u32[]{:S(2)}) copy-start(f32[192]{0:T(256)} %convert_reduce_fusion.1) | copy-start | bytes 2308
  331.4 7.6 %copy-start.24 = (f32[8,1,96]{2,0,1:T(8,128)S(1)}, f32[8,1,96]{2,0,1:T(8,128)}, u32[]{:S(2)}) copy-start(f32[8,1,96]{2,0,1:T(8,128)} %stack_reshape_unstack.18) | copy-start | bytes 9220
  331.5 7.6 %copy-start.25 = (f32[8,1,96]{2,0,1:T(8,128)S(1)}, f32[8,1,96]{2,0,1:T(8,128)}, u32[]{:S(2)}) copy-start(f32[8,1,96]{2,0,1:T(8,128)} %stack_reshape_unstack.19) | copy-start | bytes 9220
  331.5 7.6 %copy-start.26 = (f32[8,1,96]{2,0,1:T(8,128)S(1)}, f32[8,1,96]{2,0,1:T(8,128)}, u32[]{:S(2)}) copy-start(f32[8,1,96]{2,0,1:T(8,128)} %stack_reshape_unstack.20) | copy-start | bytes 9220
  331.5 7.6 %copy-start.27 = (f32[8,1,96]{2,0,1:T(8,128)S(1)}, f32[8,1,96]{2,0,1:T(8,128)}, u32[]{:S(2)}) copy-start(f32[8,1,96]{2,0,1:T(8,128)} %stack_reshape_unstack.21) | copy-start | bytes 9220
  331.5 7.6 %copy-start.28 = (f32[8,1,96]{2,0,1:T(8,128)S(1)}, f32[8,1,96]{2,0,1:T(8,128)}, u32[]{:S(2)}) copy-start(f32[8,1,96]{2,0,1:T(8,128)} %stack_reshape_unstack.22) | copy-start | bytes 9220
  331.5 7.6 %copy-start.29 = (f32[8,1,96]{2,0,1:T(8,128)S(1)}, f32[8,1,96]{2,0,1:T(8,128)}, u32[]{:S(2)}) copy-start(f32[8,1,96]{2,0,1:T(8,128)} %stack_reshape_unstack.23) | copy-start | bytes 9220
  447.3 3.3 copy-start.31
  447.4 3.8 copy-start.9
  456.4 2.9 copy-start.10
  456.4 2.9 copy-start.11
  456.4 2.9 copy-start.12
  456.4 2.9 copy-start.13
  (12 other events, 22.5 us)

commit v4 on v3

--- a/solution.py
+++ b/solution.py
@@ -79,6 +79,7 @@
                    jax.ShapeDtypeStruct((heads * HD, total), bf),
                    jax.ShapeDtypeStruct((heads, total), f32)],
         scratch_shapes=[pltpu.VMEM((heads * HD, bq), f32), pltpu.VMEM((2, heads, bq), f32)],
+        cost_estimate=pl.CostEstimate(flops=8 * heads * HD * total * total, bytes_accessed=8 * heads * HD * total, transcendentals=0),
         name="attn_fwd",
     )(starts, qT, k3, vT)
 
@@ -190,104 +191,61 @@
 SHARE = 80
 
 
-def gather_kernel(a_ref, b_ref, t_ref, g_ref, q_ref, x_ref, send, recv, lsem):
+def gather_kernel(b_ref, t_ref, q_ref, x_ref, send, recv, lsem):
     z, y, x, c, along, ypeer, xpeer, cpeer = grid_peers()
     own = z * 2 + y
-    rows = a_ref.shape[0]
-    half = rows // 2
-    plain = half - 2 * SHARE
     wire = Wire(send, recv)
     spot = lambda r, d: ((z + 4 - d) % 4) * 2 + (y if r == 0 else 1 - y)
-    base, other = half * c, half * (1 - c)
-    nspan = pl.ds(pl.multiple_of(base, 16), plain)
-    dspan = pl.ds(pl.multiple_of(base + plain + SHARE * x, 16), SHARE)
-    xspan = pl.ds(pl.multiple_of(base + plain + SHARE * (1 - x), 16), SHARE)
-    pn = pl.ds(pl.multiple_of(other, 16), plain)
-    pd = pl.ds(pl.multiple_of(other + plain + SHARE * x, 16), SHARE)
-    px = pl.ds(pl.multiple_of(other + plain + SHARE * (1 - x), 16), SHARE)
     seq = x * 2 + c
+    half = t_ref.shape[0] // 2
+    parts = [pl.ds(0, half), pl.ds(half, half)]
     locals_ = [
-        pltpu.make_async_copy(a_ref, g_ref.at[own], lsem.at[0]),
-        pltpu.make_async_copy(b_ref, q_ref.at[own], lsem.at[1]),
-        pltpu.make_async_copy(t_ref, x_ref.at[seq], lsem.at[2]),
+        pltpu.make_async_copy(b_ref, q_ref.at[own], lsem.at[0]),
+        pltpu.make_async_copy(t_ref, x_ref.at[seq], lsem.at[1]),
     ]
     for copy in locals_:
         copy.start()
     greet(along[1:] + [ypeer, xpeer, cpeer])
-    S = {}
-    for name in ("zB", "zN", "zD", "yB", "yN", "yD"):
-        S[name] = [wire.slot() for _ in range(4)]
-    for name in ("cN", "cD", "cX", "xD"):
-        S[name] = [[wire.slot() for _ in range(4)] for _ in range(2)]
-    tx, tc0, tc1 = wire.slot(), wire.slot(), wire.slot()
-    wire.start(tx, t_ref, x_ref.at[seq], xpeer)
+    zB = [wire.slot() for _ in range(4)]
+    yB = [wire.slot() for _ in range(4)]
+    tx, tc1 = [wire.slot() for _ in parts], [wire.slot() for _ in parts]
+    tc0 = wire.slot()
+    for slot, part in zip(tx, parts):
+        wire.start(slot, t_ref.at[part], x_ref.at[seq, part], xpeer)
     for d in ORDER:
-        wire.start(S["zB"][d], b_ref, q_ref.at[own], along[d])
-    wire.start(S["yB"][0], b_ref, q_ref.at[own], ypeer)
-    for d in ORDER:
-        wire.start(S["zN"][d], a_ref.at[nspan], g_ref.at[own, nspan], along[d])
-    wire.start(S["yN"][0], a_ref.at[nspan], g_ref.at[own, nspan], ypeer)
-    for d in ORDER:
-        wire.start(S["zD"][d], a_ref.at[dspan], g_ref.at[own, dspan], along[d])
-    wire.start(S["yD"][0], a_ref.at[dspan], g_ref.at[own, dspan], ypeer)
+        wire.start(zB[d], b_ref, q_ref.at[own], along[d])
+    wire.start(yB[0], b_ref, q_ref.at[own], ypeer)
     wire.start(tc0, t_ref, x_ref.at[seq], cpeer)
     for d in ORDER:
         w = spot(0, d)
-        wire.arrived(S["zB"][d], q_ref.at[w], along[d])
-        wire.start(S["yB"][d], q_ref.at[w], q_ref.at[w], ypeer)
-    for d in ORDER:
-        w = spot(0, d)
-        wire.arrived(S["zN"][d], g_ref.at[w, nspan], along[d])
-        wire.start(S["yN"][d], g_ref.at[w, nspan], g_ref.at[w, nspan], ypeer)
-        wire.start(S["cN"][0][d], g_ref.at[w, nspan], g_ref.at[w, nspan], cpeer)
+        wire.arrived(zB[d], q_ref.at[w], along[d])
+        wire.start(yB[d], q_ref.at[w], q_ref.at[w], ypeer)
     xtok = (1 - x) * 2 + c
-    wire.arrived(tx, x_ref.at[xtok], xpeer)
-    wire.start(tc1, x_ref.at[xtok], x_ref.at[xtok], cpeer)
-    for d in ORDER:
-        w = spot(0, d)
-        wire.arrived(S["zD"][d], g_ref.at[w, dspan], along[d])
-        for slot, peer in ((S["yD"][d], ypeer), (S["xD"][0][d], xpeer), (S["cD"][0][d], cpeer)):
-            wire.start(slot, g_ref.at[w, dspan], g_ref.at[w, dspan], peer)
+    for i, part in enumerate(parts):
+        wire.arrived(tx[i], x_ref.at[xtok, part], xpeer)
+        wire.start(tc1[i], x_ref.at[xtok, part], x_ref.at[xtok, part], cpeer)
     for d in (0,) + ORDER:
-        w = spot(1, d)
-        wire.arrived(S["yN"][d], g_ref.at[w, nspan], ypeer)
-        wire.start(S["cN"][1][d], g_ref.at[w, nspan], g_ref.at[w, nspan], cpeer)
-        wire.arrived(S["yB"][d], q_ref.at[w], ypeer)
-    for d in (0,) + ORDER:
-        w = spot(1, d)
-        wire.arrived(S["yD"][d], g_ref.at[w, dspan], ypeer)
-        for slot, peer in ((S["xD"][1][d], xpeer), (S["cD"][1][d], cpeer)):
-            wire.start(slot, g_ref.at[w, dspan], g_ref.at[w, dspan], peer)
-    rest = [(0, d) for d in ORDER] + [(1, d) for d in (0,) + ORDER]
-    for r, d in rest:
-        w = spot(r, d)
-        wire.arrived(S["xD"][r][d], g_ref.at[w, xspan], xpeer)
-        wire.start(S["cX"][r][d], g_ref.at[w, xspan], g_ref.at[w, xspan], cpeer)
+        wire.arrived(yB[d], q_ref.at[spot(1, d)], ypeer)
     wire.arrived(tc0, x_ref.at[x * 2 + 1 - c], cpeer)
-    wire.arrived(tc1, x_ref.at[(1 - x) * 2 + 1 - c], cpeer)
-    for r, d in rest:
-        w = spot(r, d)
-        wire.arrived(S["cN"][r][d], g_ref.at[w, pn], cpeer)
-        wire.arrived(S["cD"][r][d], g_ref.at[w, pd], cpeer)
-        wire.arrived(S["cX"][r][d], g_ref.at[w, px], cpeer)
+    for i, part in enumerate(parts):
+        wire.arrived(tc1[i], x_ref.at[(1 - x) * 2 + 1 - c, part], cpeer)
     wire.drain()
     for copy in locals_:
         copy.wait()
 
 
-def gather_inputs(a, b, tokens):
-    slots = 59 + 3 + 12
+def gather_inputs(b, tokens):
+    slots = 13
     hbm = pl.BlockSpec(memory_space=pl.ANY)
     vmem = pl.BlockSpec(memory_space=pltpu.VMEM)
     return pl.pallas_call(
         gather_kernel,
-        in_specs=[vmem] * 3, out_specs=[hbm] * 3,
-        out_shape=[jax.ShapeDtypeStruct((8,) + a.shape, a.dtype), jax.ShapeDtypeStruct((8,) + b.shape, b.dtype),
-                   jax.ShapeDtypeStruct((4,) + tokens.shape, tokens.dtype)],
-        scratch_shapes=[pltpu.SemaphoreType.DMA((slots,)), pltpu.SemaphoreType.DMA((slots,)), pltpu.SemaphoreType.DMA((3,))],
+        in_specs=[vmem] * 2, out_specs=[hbm] * 2,
+        out_shape=[jax.ShapeDtypeStruct((8,) + b.shape, b.dtype), jax.ShapeDtypeStruct((4,) + tokens.shape, tokens.dtype)],
+        scratch_shapes=[pltpu.SemaphoreType.DMA((slots,)), pltpu.SemaphoreType.DMA((slots,)), pltpu.SemaphoreType.DMA((2,))],
         compiler_params=pltpu.CompilerParams(collective_id=1, has_side_effects=True),
         name="gather_inputs",
-    )(a, b, tokens)
+    )(b, tokens)
 
 
 def add_rows(dst, parts, rows, step=16):
@@ -450,7 +408,7 @@
 
 
 def ffn_kernel(n, r, step, mixed, tokens, cot, vec, big, out, dres, ga, dO, small,
-               w_out, w_in, w_outer, stage, fb, gp, xh1, n1b, dh2, dm, du, acc, r1, lsem, gsem):
+               w_out, w_in, w_outer, stage, fb, gp, xh1, n1b, dh2, dm, du, acc, r1, lsem, gsem, send, recv):
     toks, model = tokens.shape
     wide = w_in.shape[0]
     per = n // wide
@@ -458,13 +416,32 @@
         if per:
             return ref.at[pl.ds(j * per, per), pl.ds((1 + wide) * r, wide * r)]
         return ref.at[:, pl.ds((1 + wide + j) * r, r)]
-    loads = [pltpu.make_async_copy(big.at[:, pl.ds(0, r)], w_out, lsem.at[0])]
-    for j in range(wide):
-        loads.append(pltpu.make_async_copy(big.at[:, pl.ds((1 + j) * r, r)], w_in.at[j], lsem.at[1 + j]))
-    for j in range(wide):
-        loads.append(pltpu.make_async_copy(outer_at(big, j), w_outer.at[j], lsem.at[1 + wide + j]))
-    for load in loads:
-        load.start()
+    z, y, x, c, along, ypeer, xpeer, cpeer = grid_peers()
+    wire = Wire(send, recv)
+    greet([cpeer])
+    h = r // 2
+    low = lambda size, side: pl.ds(pl.multiple_of(size * side, 16), size)
+    def place(s, side, k):
+        if k == 0:
+            return w_out.at[s, low(h, side)]
+        if k <= wide:
+            return w_in.at[k - 1, s, low(h, side)]
+        return w_outer.at[s // per, s % per, low(wide * h, side)]
+    loads = [[] for _ in range(2 + wide)]
+    for k in range(2 + wide):
+        span = pl.ds(k * h, h if k <= wide else wide * h)
+        for s in range(n):
+            slot = wire.slot()
+            load = pltpu.make_async_copy(big.at[s, span], place(s, c, k), lsem.at[slot])
+            load.start()
+            wire.start(slot, big.at[s, span], place(s, c, k), cpeer)
+            loads[k].append((load, slot, place(s, 1 - c, k)))
+
+    def ready(k):
+        for load, slot, spot in loads[k]:
+            load.wait()
+            wire.arrived(slot, spot, cpeer)
+
     stores = []
 
     def put(value_rows, place):
@@ -484,7 +461,7 @@
     row = lambda i: vec[i:i + 1, :]
     b_output, b_outer, g1, s1, g2, s2 = [row(i) for i in (2, 3, 4, 5, 6, 7)]
     small[...] = jnp.zeros_like(small)
-    loads[0].wait()
+    ready(0)
     wo = flat(w_out)
 
     def first(at):
@@ -500,7 +477,7 @@
         acc[at, :] = norm + b_outer
     chunks(toks, step, first)
     for j in range(wide):
-        loads[1 + j].wait()
+        ready(1 + j)
         wi = flat(w_in.at[j])
         bias = row(8 + j)
         def inner(at, j=j, wi=wi, bias=bias):
@@ -510,7 +487,8 @@
             fb[j, at, :] = (u * cdf).astype(bf)
             gp[j, at, :] = cdf + u * pdf
         chunks(toks, step, inner)
-        loads[1 + wide + j].wait()
+    ready(1 + wide)
+    for j in range(wide):
         wout = flat(w_outer.at[j])
         def outer(at, j=j, wout=wout):
             acc[at, :] += mm(fb[j, at, :], wout[...], 1, 0)
@@ -567,12 +545,13 @@
     put(lambda at: mm(mixed[at, :], dm[...], 1, 0), ga.at[:, pl.ds(0, r)])
     for store in stores[-stage.shape[0]:]:
         store.wait()
+    wire.drain()
 
 
 def ffn_block(mixed, tokens, cot, vec, big, step=384):
-    n, rows9, model = big.shape
+    n, half, model = big.shape
     r = model // n
-    wide = (rows9 // r - 1) // 2
+    wide = (2 * half // r - 1) // 2
     toks = tokens.shape[0]
     vmem = pl.BlockSpec(memory_space=pltpu.VMEM)
     hbm = pl.BlockSpec(memory_space=pl.ANY)
@@ -585,13 +564,14 @@
         in_specs=[vmem] * 4 + [hbm],
         out_specs=[vmem, vmem, hbm, vmem, vmem],
         out_shape=[jax.ShapeDtypeStruct((toks, model), bf), jax.ShapeDtypeStruct((toks, model), f32),
-                   jax.ShapeDtypeStruct(big.shape, bf), jax.ShapeDtypeStruct((model, toks), bf),
+                   jax.ShapeDtypeStruct((n, 2 * half, model), bf), jax.ShapeDtypeStruct((model, toks), bf),
                    jax.ShapeDtypeStruct((16, model), f32)],
         scratch_shapes=[V((n, r, model), bf), V((wide, n, r, model), bf), V((wide,) + ohold, bf), V((4, model, model), bf),
                         sq(bf, wide), sq(f32, wide), sq(f32), sq(bf), sq(f32), sq(bf), sq(bf), sq(f32),
-                        V((toks, 128), f32), pltpu.SemaphoreType.DMA((1 + 2 * wide,)), pltpu.SemaphoreType.DMA((4,))],
-        compiler_params=pltpu.CompilerParams(vmem_limit_bytes=67043328),
-        cost_estimate=pl.CostEstimate(flops=2 * toks * model * model * (3 + 6 * wide), bytes_accessed=4 * big.size, transcendentals=2 * toks * model * wide),
+                        V((toks, 128), f32), pltpu.SemaphoreType.DMA(((2 + wide) * n,)), pltpu.SemaphoreType.DMA((4,)),
+                        pltpu.SemaphoreType.DMA(((2 + wide) * n,)), pltpu.SemaphoreType.DMA(((2 + wide) * n,))],
+        compiler_params=pltpu.CompilerParams(collective_id=3, has_side_effects=True, vmem_limit_bytes=67043328),
+        cost_estimate=pl.CostEstimate(flops=2 * toks * model * model * (3 + 6 * wide), bytes_accessed=8 * n * half * model, transcendentals=2 * toks * model * wide),
         name="ffn_block",
     )(mixed, tokens, cot, vec, big)
 
@@ -618,12 +598,6 @@
 
 def chips_of_two_by_four():
     return lax.axis_size("wshard") == 8 and lax.axis_size("seq") == 4
-
-
-def gather_parts(a, b, tokens):
-    if chips_of_two_by_four():
-        return gather_inputs(a, b, tokens)
-    return lax.all_gather(a, "wshard"), lax.all_gather(b, "wshard"), lax.all_gather(tokens, "seq")
 
 
 def reduce_parts(ga, gb, dx, sm):
@@ -707,11 +681,20 @@
     smalls = (b_query, b_value, b_output, b_outer, gain_first, bias_first, gain_second, bias_second)
     small_cols = jnp.stack(smalls + tuple(b_inner.reshape(wide, rows)), axis=1)
     cols_n = small_cols.shape[1]
-    a = jnp.concatenate(
-        [w_output, w_inner.reshape(rows, wide, model).transpose(1, 0, 2).reshape(wide * rows, model), w_outer], axis=0
-    )
     b = jnp.concatenate([own(w_query), own(w_key), own(w_value), jnp.pad(small_cols, ((0, 0), (0, HD - cols_n)))], axis=1)
-    big, side, stream = gather_parts(a, b, tokens)
+    fast = chips_of_two_by_four()
+
+    def packed(share, part):
+        cut = lambda w: lax.dynamic_slice_in_dim(w, w.shape[0] // share * part, w.shape[0] // share, 0)
+        inner = cut(w_inner).reshape(rows // share, wide, model).transpose(1, 0, 2).reshape(-1, model)
+        return jnp.concatenate([cut(w_output), inner, cut(w_outer)], axis=0)
+
+    if fast:
+        big = lax.all_gather(packed(2, seq_i % 2), "wshard")
+        side, stream = gather_inputs(b, tokens)
+    else:
+        big = lax.all_gather(packed(1, 0), "wshard")
+        side, stream = lax.all_gather(b, "wshard"), lax.all_gather(tokens, "seq")
     stream = stream.reshape(-1, model)
     side = side.reshape(model, -1)
     w_own = side[:, :3 * width]
@@ -734,8 +717,10 @@
     mixed = lax.all_to_all(mixT, "seq", split_axis=1, concat_axis=0, tiled=True)
 
     vec = jnp.concatenate([vectors[:8], bias_inner.reshape(wide, model), jnp.zeros((4, model), f32)], axis=0)
-    feed = ffn_block if chips_of_two_by_four() else ffn_plain
-    layer_result, d_resid, ga, d_mixed, sums = feed(mixed, tokens, cotangent, vec, big)
+    if fast:
+        layer_result, d_resid, ga, d_mixed, sums = ffn_block(mixed, tokens, cotangent, vec, big)
+    else:
+        layer_result, d_resid, ga, d_mixed, sums = ffn_plain(mixed, tokens, cotangent, vec, big)
     doT = lax.all_to_all(d_mixed, "seq", split_axis=0, concat_axis=1, tiled=True)
 
     dqT, dk3, dv3 = attn_bwd(starts, qT, q3, k3, kT, v3, doT, by_token(doT), oT, lse, 256, 512)

time: 455 us -> 419 us (0.921); the launches traced: 460 us -> 417 us
  Pallas kernels: 351 us -> 288 us
  between operations: 1.33 us -> 14.9 us
  matrix products: 23.7 us -> 29 us
    pallas_call x1, Pallas kernels: 86.3 us -> 35.7 us  [gather_inputs(): pl.pallas_call(gather_kernel, in_specs=[vmem] * 2, out_specs=[hbm] * 2, o...]
    pallas_call x1, Pallas kernels: 48.1 us -> 39.3 us  [attn_bwd(): pl.pallas_call(functools.partial(bwd_kernel, heads, bq, bk), grid=(total...]
    pallas_call x1, Pallas kernels: 48.2 us -> 40.1 us  [attn_fwd(): pl.pallas_call(functools.partial(fwd_kernel, heads, bq, bk), grid=(total...]
    dot_general x5, matrix products: 23.7 us -> 29 us  [contract(): lax.dot_general(left_in, right_in, (((left_dim,), (right_dim,)), ((), ())...]
  transfers between devices with their start and end apart: 2 -> 3, of which waited for: 2 -> 2; matrix products, arithmetic and copies ran while one was open for 2% -> 9% of each run, Pallas kernels for 0% -> 18%
where the time goes in v4:
time: 419 us; the launch traced here: 417 us
  Pallas kernels  288 us (69%)
  local copies, waits for them, and re-layouts  41.6 us (10%)
  matrix products  29 us (7%)
  waiting for transfers between devices  21.7 us (5%)
  between operations  14.9 us (4%)
  other arithmetic  13 us (3%)
  starting transfers between devices  8.24 us (2%)
    pallas_call x1, Pallas kernels, reduce_grads(): pl.pallas_call(reduce_kernel, in_specs=[vmem] * 4, out_specs=[vmem] * 5,...  110 us
    pallas_call x1, Pallas kernels, ffn_block(): pl.pallas_call(functools.partial(ffn_kernel, n, r, step), in_specs=[vmem]...  63.5 us
    pallas_call x1, Pallas kernels, attn_fwd(): pl.pallas_call(functools.partial(fwd_kernel, heads, bq, bk), grid=(total...  40.1 us
    pallas_call x1, Pallas kernels, attn_bwd(): pl.pallas_call(functools.partial(bwd_kernel, heads, bq, bk), grid=(total...  39.3 us
    pallas_call x1, Pallas kernels, gather_inputs(): pl.pallas_call(gather_kernel, in_specs=[vmem] * 2, out_specs=[hbm] * 2, o...  35.7 us
    dot_general x5, matrix products, contract(): lax.dot_general(left_in, right_in, (((left_dim,), (right_dim,)), ((), ())...  29 us
    all_to_all x1, waiting for transfers between devices, shards(): mixed = lax.all_to_all(mixT, 'seq', split_axis=1, concat_axis=0, tiled=True)  14.9 us
    reshape x5, local copies, waits for them, and re-layouts, by_token(): return arr.reshape(heads, HD, -1).transpose(0, 2, 1)  10.6 us
  transfers between devices with their start and end apart: 3, of which 2 were waited for; matrix products, arithmetic and copies ran while one was open for 9% of the time, Pallas kernels for 18%

profile of v4, /device:TPU:0, one launch (start us, length us, event | category | flops | bytes accessed | tf_op | source)
XLA Modules:
  0.0 416.7 jit_solution(7665225827704659718)
XLA Ops:
  15.4 35.7 %gather_inputs.1 = (bf16[8,96,640]{2,1,0:T(8,128)(2,1)}, bf16[4,768,768]{2,1,0:T(8,128)(2,1)}) custom-call(bf16[96,640]{1,0:T(8,128)(2,1)} %fusion.10.b_ref, bf16[768,768]{1,0:T(8,128)(2,1)} %tokens.1), custom_call_target="tpu_custom_call" | custom-call | tf_op jit(solution)/shard_map/gather_inputs/pallas_call | solution.py:241
  52.3 4.5 %convolution_convert_fusion.1.kT = bf16[192,3072]{1,0:T(8,128)(2,1)S(1)} fusion(bf16[3072,768]{1,0:T(8,128)(2,1)} %bitcast.152, bf16[768,640]{1,0:T(8,128)(2,1)} %bitcast.131), kind=kOutput, calls=%fused_computation.6 | convolution fusion | flops 906559488 | bytes 6291456 | tf_op jit(solution)/shard_map/dot_general | solution.py:591
  56.8 2.4 copy.120
  59.3 5.8 %fusion.1.vT = bf16[192,3072]{1,0:T(8,128)(2,1)} fusion(bf16[3072,768]{1,0:T(8,128)(2,1)} %bitcast.153, f32[192]{0:T(256)S(1)} %bitcast.142, bf16[768,640]{1,0:T(8,128)(2,1)S(1)} %bitcast.133), kind=kOutput, calls=%fused_computation.5 | convolution fusion | flops 907149312 | bytes 6292480 | tf_op jit(solution)/shard_map/dot_general | solution.py:591
  65.1 5.2 %fusion.2.qT = bf16[192,3072]{1,0:T(8,128)(2,1)} fusion(bf16[3072,768]{1,0:T(8,128)(2,1)} %bitcast.154, f32[192]{0:T(256)S(1)} %bitcast.141, bf16[768,640]{1,0:T(8,128)(2,1)S(1)} %bitcast.134), kind=kOutput, calls=%fused_computation.7 | convolution fusion | flops 907739136 | bytes 6292480 | tf_op jit(solution)/shard_map/dot_general | solution.py:591
  70.4 40.1 %attn_fwd.1 = (f32[192,3072]{1,0:T(8,128)}, bf16[192,3072]{1,0:T(8,128)(2,1)}, f32[3,3072]{1,0:T(4,128)}) custom-call(s32[1,8]{1,0:T(1,128)} %starts.3, bf16[192,3072]{1,0:T(8,128)(2,1)} %fusion.2.qT, bf16[3,3072,64]{2,1,0:T(8,128)(2,1)} %bitcast.108, bf16[192,3072]{1,0:T(8,128)(2,1)} %fusion.1.vT), custom_call_target="tpu_custom_call" | custom-call | flops 14495514624 | bytes 4718592 | tf_op jit(solution)/shard_map/attn_fwd/pallas_call | solution.py:68
  110.5 2.4 copy.143
  112.8 4.5 %all-to-all-start = ((bf16[192,4,768]{2,0,1:T(8,128)(2,1)}), bf16[192,4,768]{2,0,1:T(8,128)(2,1)}, u32[]{:S(2)}, u32[]{:S(2)}) async-start(bf16[192,4,768]{2,0,1:T(8,128)(2,1)} %bitcast.102), calls=%async_computation | async-start | bytes 2359296 | tf_op jit(solution)/shard_map/all_to_all | solution.py:717
  118.4 14.9 %all-to-all-done = bf16[192,4,768]{2,0,1:T(8,128)(2,1)} async-done(((bf16[192,4,768]{2,0,1:T(8,128)(2,1)}), bf16[192,4,768]{2,0,1:T(8,128)(2,1)}, u32[]{:S(2)}, u32[]{:S(2)}) %all-to-all-start) | async-done | bytes 1179680 | tf_op jit(solution)/shard_map/all_to_all | solution.py:717
  133.3 63.5 %ffn_block.1 = (bf16[768,768]{1,0:T(8,128)(2,1)}, f32[768,768]{1,0:T(8,128)}, bf16[8,864,768]{2,1,0:T(8,128)(2,1)}, bf16[768,768]{1,0:T(8,128)(2,1)}, f32[16,768]{1,0:T(8,128)}) custom-call(bf16[768,768]{1,0:T(8,128)(2,1)} %bitcast.20.mixed, bf16[768,768]{1,0:T(8,128)(2,1)} %tokens.1, bf16[768,768]{1,0:T(8,128)(2,1)} %cot.1, ...), custom_call_target="tpu_custom_call" | custom-call | flops 24461180928 | bytes 21233664 | tf_op jit(solution)/shard_map/ffn_block/pallas_call | solution.py:562
  196.8 3.7 all-to-all-start.1
  200.5 2.4 copy.125
  202.9 2.5 copy.124
  209.5 6.8 %all-to-all-done.1 = bf16[4,192,768]{2,1,0:T(8,128)(2,1)S(1)} async-done(((bf16[4,192,768]{2,1,0:T(8,128)(2,1)}), bf16[4,192,768]{2,1,0:T(8,128)(2,1)S(1)}, u32[]{:S(2)}, u32[]{:S(2)}) %all-to-all-start.1) | async-done | bytes 1179680 | tf_op jit(solution)/shard_map/all_to_all | solution.py:724
  218.1 2.4 copy.128
  221.7 39.3 %attn_bwd.1 = (bf16[192,3072]{1,0:T(8,128)(2,1)}, bf16[3,3072,64]{2,1,0:T(8,128)(2,1)}, bf16[3,3072,64]{2,1,0:T(8,128)(2,1)}) custom-call(s32[1,8]{1,0:T(1,128)} %starts.3, bf16[192,3072]{1,0:T(8,128)(2,1)} %fusion.2.qT, bf16[3,3072,64]{2,1,0:T(8,128)(2,1)} %bitcast.111, bf16[3,3072,64]{2,1,0:T(8,128)(2,1)} %bitcast.109, bf16[192,3072]{1,0:T(8,128)(2,1)} %copy-done.2, ...), custom_call_target="tpu_custom_call" | custom-call | tf_op jit(solution)/shard_map/attn_bwd/pallas_call | solution.py:130
  260.9 2.8 convert_reduce_fusion
  264.6 2.8 copy.129
  267.4 2.1 copy.130
  269.5 8.2 %convolution_convert_fusion = bf16[3072,768]{1,0:T(8,128)(2,1)} fusion(bf16[192,3072]{1,0:T(8,128)(2,1)} %bitcast.122, bf16[192,3072]{1,0:T(8,128)(2,1)S(1)} %bitcast.120, bf16[192,3072]{1,0:T(8,128)(2,1)} %get-tuple-element.43, bf16[768,640]{1,0:T(8,128)(2,1)} %bitcast.132), kind=kOutput, calls=%fused_computation | convolution fusion | flops 2730885120 | bytes 9240576 | tf_op jit(solution)/shard_map/dot_general | solution.py:591
  277.8 5.3 %fusion.4 = bf16[768,576]{0,1:T(8,128)(2,1)S(1)} fusion(bf16[3072,768]{1,0:T(8,128)(2,1)} %bitcast.155, bf16[192,3072]{1,0:T(8,128)(2,1)S(1)} %bitcast.123, bf16[192,3072]{1,0:T(8,128)(2,1)S(1)} %bitcast.121, bf16[192,3072]{1,0:T(8,128)(2,1)S(1)} %copy-done.9), kind=kOutput, calls=%fused_computation.12 | convolution fusion | flops 2728968192 | bytes 9142272 | tf_op jit(solution)/shard_map/dot_general | solution.py:591
  286.1 109.7 %reduce_grads.1 = (bf16[864,768]{1,0:T(8,128)(2,1)}, bf16[4,96,576]{2,1,0:T(8,128)(2,1)}, bf16[768,768]{1,0:T(8,128)(2,1)}, bf16[768,768]{1,0:T(8,128)(2,1)}, f32[16,128]{1,0:T(8,128)}) custom-call(bf16[4,2,864,768]{3,2,1,0:T(8,128)(2,1)} %bitcast.106, bf16[4,2,96,576]{3,2,1,0:T(8,128)(2,1)} %bitcast.117, bf16[2,2,768,768]{3,2,1,0:T(8,128)(2,1)} %bitcast.113, ...), custom_call_target="tpu_custom_call" | custom-call | tf_op jit(solution)/shard_map/reduce_grads/pallas_call | solution.py:382
  395.8 2.2 fusion.13
  401.4 3.3 add_add_fusion
  (149 shorter events, 29.4 us)
Async XLA Ops:
  7.2 4.2 %copy-start.33 = (bf16[384]{0:T(512)(128)(2,1)S(1)}, bf16[384]{0:T(512)(128)(2,1)}, u32[]{:S(2)}) copy-start(bf16[384]{0:T(512)(128)(2,1)} %param.30) | copy-start | bytes 2308
  7.2 4.3 %copy-start.35 = (bf16[96]{0:T(256)(128)(2,1)S(1)}, bf16[96]{0:T(256)(128)(2,1)}, u32[]{:S(2)}) copy-start(bf16[96]{0:T(256)(128)(2,1)} %param.27) | copy-start | bytes 580
  7.2 4.3 %copy-start.36 = (bf16[96]{0:T(256)(128)(2,1)S(1)}, bf16[96]{0:T(256)(128)(2,1)}, u32[]{:S(2)}) copy-start(bf16[96]{0:T(256)(128)(2,1)} %param.28) | copy-start | bytes 580
  7.2 4.3 %copy-start.37 = (bf16[96]{0:T(256)(128)(2,1)S(1)}, bf16[96]{0:T(256)(128)(2,1)}, u32[]{:S(2)}) copy-start(bf16[96]{0:T(256)(128)(2,1)} %param.29) | copy-start | bytes 580
  7.2 4.3 %copy-start.38 = (bf16[96]{0:T(256)(128)(2,1)S(1)}, bf16[96]{0:T(256)(128)(2,1)}, u32[]{:S(2)}) copy-start(bf16[96]{0:T(256)(128)(2,1)} %param.31) | copy-start | bytes 580
  7.2 4.3 %copy-start.39 = (bf16[96]{0:T(256)(128)(2,1)S(1)}, bf16[96]{0:T(256)(128)(2,1)}, u32[]{:S(2)}) copy-start(bf16[96]{0:T(256)(128)(2,1)} %param.32) | copy-start | bytes 580
  7.3 4.3 %copy-start.40 = (bf16[96]{0:T(256)(128)(2,1)S(1)}, bf16[96]{0:T(256)(128)(2,1)}, u32[]{:S(2)}) copy-start(bf16[96]{0:T(256)(128)(2,1)} %param.33) | copy-start | bytes 580
  7.3 4.3 %copy-start.41 = (bf16[96]{0:T(256)(128)(2,1)S(1)}, bf16[96]{0:T(256)(128)(2,1)}, u32[]{:S(2)}) copy-start(bf16[96]{0:T(256)(128)(2,1)} %param.34) | copy-start | bytes 580
  7.3 4.3 %copy-start.42 = (bf16[96]{0:T(256)(128)(2,1)S(1)}, bf16[96]{0:T(256)(128)(2,1)}, u32[]{:S(2)}) copy-start(bf16[96]{0:T(256)(128)(2,1)} %param.35) | copy-start | bytes 580
  7.3 126.0 %all-gather.3.cloned.1.call-start = ((), (), s32[]{:S(2)}) async-start(), calls=%async_computation.2 | async-start | bytes 5971968 | tf_op jit(solution)/shard_map/all_gather | solution.py:693
  56.8 8.3 %copy-start.2 = (bf16[192,3072]{1,0:T(8,128)(2,1)}, bf16[192,3072]{1,0:T(8,128)(2,1)S(1)}, u32[]{:S(2)}) copy-start(bf16[192,3072]{1,0:T(8,128)(2,1)S(1)} %convolution_convert_fusion.1.kT) | copy-start | bytes 3538948
  112.8 20.4 %all-to-all-start = ((bf16[192,4,768]{2,0,1:T(8,128)(2,1)}), bf16[192,4,768]{2,0,1:T(8,128)(2,1)}, u32[]{:S(2)}, u32[]{:S(2)}) async-start(bf16[192,4,768]{2,0,1:T(8,128)(2,1)} %bitcast.102), calls=%async_computation | async-start | bytes 2359296 | tf_op jit(solution)/shard_map/all_to_all | solution.py:717
  196.8 19.5 %all-to-all-start.1 = ((bf16[4,192,768]{2,1,0:T(8,128)(2,1)}), bf16[4,192,768]{2,1,0:T(8,128)(2,1)S(1)}, u32[]{:S(2)}, u32[]{:S(2)}) async-start(bf16[4,192,768]{2,1,0:T(8,128)(2,1)} %bitcast.124), calls=%async_computation.1 | async-start | bytes 2359296 | tf_op jit(solution)/shard_map/all_to_all | solution.py:724
  269.5 8.2 %copy-start.6 = (bf16[3,64,3072]{2,1,0:T(8,128)(2,1)S(1)}, bf16[3,64,3072]{2,1,0:T(8,128)(2,1)}, u32[]{:S(2)}) copy-start(bf16[3,64,3072]{2,1,0:T(8,128)(2,1)} %copy.130) | copy-start | bytes 3538948
  269.5 8.2 %copy-start.9 = (bf16[192,3072]{1,0:T(8,128)(2,1)S(1)}, bf16[192,3072]{1,0:T(8,128)(2,1)}, u32[]{:S(2)}) copy-start(bf16[192,3072]{1,0:T(8,128)(2,1)} %get-tuple-element.43) | copy-start | bytes 3538948
  277.7 5.3 %copy-start.31 = (f32[3,64]{1,0:T(4,128)S(1)}, f32[3,64]{1,0:T(4,128)}, u32[]{:S(2)}) copy-start(f32[3,64]{1,0:T(4,128)} %convert_reduce_fusion) | copy-start | bytes 2308
  277.7 6.0 %copy-start.34 = (f32[192]{0:T(256)S(1)}, f32[192]{0:T(256)}, u32[]{:S(2)}) copy-start(f32[192]{0:T(256)} %convert_reduce_fusion.1) | copy-start | bytes 2308
  277.7 7.6 %copy-start.25 = (f32[8,1,96]{2,0,1:T(8,128)S(1)}, f32[8,1,96]{2,0,1:T(8,128)}, u32[]{:S(2)}) copy-start(f32[8,1,96]{2,0,1:T(8,128)} %stack_reshape_unstack.18) | copy-start | bytes 9220
  277.7 7.6 %copy-start.26 = (f32[8,1,96]{2,0,1:T(8,128)S(1)}, f32[8,1,96]{2,0,1:T(8,128)}, u32[]{:S(2)}) copy-start(f32[8,1,96]{2,0,1:T(8,128)} %stack_reshape_unstack.19) | copy-start | bytes 9220
  277.7 7.6 %copy-start.27 = (f32[8,1,96]{2,0,1:T(8,128)S(1)}, f32[8,1,96]{2,0,1:T(8,128)}, u32[]{:S(2)}) copy-start(f32[8,1,96]{2,0,1:T(8,128)} %stack_reshape_unstack.20) | copy-start | bytes 9220
  277.8 7.6 %copy-start.28 = (f32[8,1,96]{2,0,1:T(8,128)S(1)}, f32[8,1,96]{2,0,1:T(8,128)}, u32[]{:S(2)}) copy-start(f32[8,1,96]{2,0,1:T(8,128)} %stack_reshape_unstack.21) | copy-start | bytes 9220
  277.8 7.6 %copy-start.29 = (f32[8,1,96]{2,0,1:T(8,128)S(1)}, f32[8,1,96]{2,0,1:T(8,128)}, u32[]{:S(2)}) copy-start(f32[8,1,96]{2,0,1:T(8,128)} %stack_reshape_unstack.22) | copy-start | bytes 9220
  277.8 7.6 %copy-start.30 = (f32[8,1,96]{2,0,1:T(8,128)S(1)}, f32[8,1,96]{2,0,1:T(8,128)}, u32[]{:S(2)}) copy-start(f32[8,1,96]{2,0,1:T(8,128)} %stack_reshape_unstack.23) | copy-start | bytes 9220
  395.8 3.8 copy-start.10
  (22 other events, 53.7 us)
Sparse Core Ops, SparseCore 0:
  11.5 97.0 all-gather.2
